TPU v7x, 32 devices: a whole 2x2x4 slice. The times are simulated.
32 devices in a mesh: rep: 4 (over z), shard: 8 (over y, x, core).
Axes of the slice: x: 2, y: 2, z: 4, core: 2. Of those that a mesh axis runs over, the one named last changes fastest.
Arguments:
- tokens: bfloat16 [16384, 1024], P(('rep', 'shard')), may hold values from -6 to 6
- cotangent: bfloat16 [16384, 1024], P(('rep', 'shard')), may hold values from -6 to 6
- seq_lengths: int32 [32, 4], P(('rep', 'shard')), may hold values from 1 to 256, 512 in all within a row
- pack_order: int32 [16384], P(('rep', 'shard')), may hold values from 0 to 511, as said below
- unpack_order: int32 [16384], P(('rep', 'shard')), may hold values from 0 to 511, as said below
- expert_ids: int32 [16384, 8], P(('rep', 'shard')), may hold values from 0 to 15, all different within a row; in each aligned block of 512 rows (0 to 511, 512 to 1023, ...) at most 384 rows name the same one
- gates: float32 [16384, 8], P(('rep', 'shard')), may hold values from 0.06 to 0.19
- first_gain: bfloat16 [1024], P('shard'), may hold values from 0.5 to 1.5
- query_weight: bfloat16 [1024, 1024], P('shard'), may hold values from -0.1875 to 0.1875
- key_matrix: bfloat16 [1024, 512], P('shard'), may hold values from -0.1875 to 0.1875
- value_matrix: bfloat16 [1024, 512], P('shard'), may hold values from -0.1875 to 0.1875
- output_weight: bfloat16 [1024, 1024], P('shard'), may hold values from -0.75 to 0.75
- second_gain: bfloat16 [1024], P('shard'), may hold values from 0.5 to 1.5
- gate_weight: bfloat16 [16, 1024, 512], P('shard'), may hold values from -0.1875 to 0.1875
- up_weight: bfloat16 [16, 1024, 512], P('shard'), may hold values from -0.1875 to 0.1875
- down_weight: bfloat16 [16, 512, 1024], P('shard'), may hold values from -1 to 1
Outputs:
- out_tokens: bfloat16 [16384, 1024], P(('rep', 'shard'))
- delta_tokens: bfloat16 [16384, 1024], P(('rep', 'shard'))
- delta_first: float32 [1024], P('shard')
- delta_query: float32 [1024, 1024], P('shard')
- delta_key: float32 [1024, 512], P('shard')
- delta_value: float32 [1024, 512], P('shard')
- delta_output: float32 [1024, 1024], P('shard')
- delta_second: float32 [1024], P('shard')
- delta_gate: float32 [16, 1024, 512], P('shard')
- delta_up: float32 [16, 1024, 512], P('shard')
- delta_down: float32 [16, 512, 1024], P('shard')
Inputs may be any that keep to these rules, and one draw needn't show every extreme that they name: `seq_lengths`: each row sums to 512, and its longest entry is exactly 256. `pack_order`: the 512 entries of each pack form a permutation. `unpack_order`: the 512 entries of each pack form the inverse of that pack's permutation in pack_order. `expert_ids`: A row names 8 different experts; among the 512 rows of one pack no expert is named more than 384 times, and in some pack one expert is named exactly 384 times.
All inputs are finite; a program needn't handle non-finite values.
Results may differ from a plain program's by a relative error of at most 0.02.
Values may be sent and summed in bfloat16 or wider, within the bound.
A program may use at most 256 MiB of HBM per device.

v0:
```python
import jax
import jax.numpy as jnp
from jax import lax
from jax.sharding import PartitionSpec as P

QUERY_HEADS = 16
KEY_VALUE_HEADS = 8
HEAD_SIZE = 64


EPS = 1e-05
THETA = 10000.0


def rope_tables(place, size):
    half = size // 2
    freq = THETA ** (-2.0 * jnp.arange(half, dtype=jnp.float32) / size)
    angle = place.astype(jnp.float32)[:, None] * freq[None, :]
    return (jnp.cos(angle), jnp.sin(angle))


def rotary_apply(heads, cosine_table, sine_table):
    half = heads.shape[-1] // 2
    first = heads[..., :half]
    second = heads[..., half:]
    along = cosine_table[:, None, :]
    across = sine_table[:, None, :]
    return jnp.concatenate(
        [first * along - second * across, second * along + first * across], axis=-1
    )


def rotary_inverse(heads, cosine_table, sine_table):
    half = heads.shape[-1] // 2
    first = heads[..., :half]
    second = heads[..., half:]
    along = cosine_table[:, None, :]
    across = sine_table[:, None, :]
    return jnp.concatenate(
        [first * along + second * across, second * along - first * across], axis=-1
    )


def segment_info(lengths, group_count):
    ends = jnp.cumsum(lengths)
    starts = ends - lengths
    place = jnp.arange(group_count, dtype=jnp.int32)
    inside = ((place[:, None] >= starts[None, :]) & (place[:, None] < ends[None, :])).astype(
        jnp.int32
    )
    segment = jnp.sum(inside * jnp.arange(lengths.shape[0], dtype=jnp.int32)[None, :], axis=1)
    offset = jnp.sum(inside * starts[None, :], axis=1)
    return (segment, place - offset)


def masked_scores(query_block, key_rows, start, segment, scale):
    width = query_block.shape[0]
    scores = (
        jnp.einsum("igzd,jgd->gzij", query_block, key_rows, preferred_element_type=jnp.float32)
        * scale
    )
    rows = start + jnp.arange(width, dtype=jnp.int32)
    columns = jnp.arange(key_rows.shape[0], dtype=jnp.int32)
    allowed = (segment[:, None] == segment[None, :]) & (columns[None, :] <= rows[:, None])
    return jnp.where(allowed, scores, -1e30)


def block_starts(group_count):
    width = min(512, group_count)
    blocks = group_count // width
    return (width, blocks, jnp.arange(blocks, dtype=jnp.int32) * width)


def attend(query_rows, key_rows, value_rows, segment, scale):
    group_count = query_rows.shape[0]
    width, blocks, starts = block_starts(group_count)
    grouped = query_rows.reshape((blocks, width) + query_rows.shape[1:])

    def one_block(piece):
        query_block, start = piece
        scores = masked_scores(query_block, key_rows, start, segment, scale)
        largest = jnp.max(scores, axis=-1, keepdims=True)
        powers = jnp.exp(scores - largest)
        totals = jnp.sum(powers, axis=-1, keepdims=True)
        weights = (powers / totals).astype(jnp.bfloat16)
        mixed = jnp.einsum(
            "gzij,jgd->igzd", weights, value_rows, preferred_element_type=jnp.float32
        )
        return (mixed.astype(jnp.bfloat16), (largest + jnp.log(totals))[..., 0])

    mixed, logsum = lax.map(one_block, (grouped, starts))
    return (mixed.reshape(group_count, -1), logsum)


def attend_back(query_rows, key_rows, value_rows, segment, scale, logsum, mixed_slope):
    group_count = query_rows.shape[0]
    width, blocks, starts = block_starts(group_count)
    grouped = query_rows.reshape((blocks, width) + query_rows.shape[1:])
    slope_blocks = mixed_slope.reshape(grouped.shape)

    def one_block(piece):
        query_block, slope_block, logsum_block, start = piece
        scores = masked_scores(query_block, key_rows, start, segment, scale)
        probs = jnp.exp(scores - logsum_block[..., None])
        prob_slope = jnp.einsum(
            "igzd,jgd->gzij", slope_block, value_rows, preferred_element_type=jnp.float32
        )
        inner = jnp.sum(probs * prob_slope, axis=-1, keepdims=True)
        score_slope = (probs * (prob_slope - inner)).astype(jnp.bfloat16)
        query_slope = (
            jnp.einsum("gzij,jgd->igzd", score_slope, key_rows, preferred_element_type=jnp.float32)
            * scale
        )
        key_gradient = (
            jnp.einsum(
                "gzij,igzd->jgd", score_slope, query_block, preferred_element_type=jnp.float32
            )
            * scale
        )
        value_gradient = jnp.einsum(
            "gzij,igzd->jgd",
            probs.astype(jnp.bfloat16),
            slope_block,
            preferred_element_type=jnp.float32,
        )
        return (query_slope, key_gradient, value_gradient)

    query_slope, key_gradient, value_gradient = lax.map(
        one_block, (grouped, slope_blocks, logsum, starts)
    )
    return (
        query_slope.reshape(group_count, -1, query_rows.shape[-1]),
        jnp.sum(key_gradient, axis=0),
        jnp.sum(value_gradient, axis=0),
    )


def norm_back(inputs, scale_rows, gain, slope):
    scaled = slope * gain
    gain_slope = jnp.sum(slope * inputs * scale_rows, axis=0)
    input_slope = scale_rows * scaled - inputs * scale_rows**3 * jnp.mean(
        inputs * scaled, axis=1, keepdims=True
    )
    return (input_slope, gain_slope)


def expert_forward(rows, gate_weight, up_weight):
    gate_act = jnp.einsum("secd,edf->secf", rows, gate_weight, preferred_element_type=jnp.float32)
    up_act = jnp.einsum("secd,edf->secf", rows, up_weight, preferred_element_type=jnp.float32)
    inner = (jax.nn.silu(gate_act) * up_act).astype(jnp.bfloat16)
    return (gate_act, up_act, inner)


def local(
    tokens,
    cotangent,
    seq_lengths,
    pack_order,
    unpack_order,
    expert_ids,
    gates,
    first_gain,
    query_weight,
    key_matrix,
    value_matrix,
    output_weight,
    second_gain,
    gate_weight,
    up_weight,
    down_weight,
):
    shards = lax.axis_size("shard")
    group_count = tokens.shape[0]
    width = tokens.shape[1]
    arrived = (
        lax.all_to_all(tokens, "shard", split_axis=0, concat_axis=0, tiled=True),
        lax.all_to_all(cotangent, "shard", split_axis=0, concat_axis=0, tiled=True),
    )
    inputs_low = arrived[0][pack_order]
    slope_low = arrived[1][pack_order]
    inputs = inputs_low.astype(jnp.float32)
    slopes = slope_low.astype(jnp.float32)
    gathered = (
        lax.all_gather(first_gain, "shard", axis=0, tiled=True),
        lax.all_gather(query_weight, "shard", axis=0, tiled=True),
        lax.all_gather(key_matrix, "shard", axis=0, tiled=True),
        lax.all_gather(value_matrix, "shard", axis=0, tiled=True),
        lax.all_gather(output_weight, "shard", axis=0, tiled=True),
        lax.all_gather(second_gain, "shard", axis=0, tiled=True),
    )
    gain_one, full_query, full_key, full_value, full_output, gain_two = gathered
    gain_one = gain_one.astype(jnp.float32)
    gain_two = gain_two.astype(jnp.float32)
    segment, place = segment_info(seq_lengths[0], group_count)
    cosine_table, sine_table = rope_tables(place, HEAD_SIZE)
    scale = HEAD_SIZE ** (-0.5)
    head_groups = QUERY_HEADS // KEY_VALUE_HEADS
    first_scale = lax.rsqrt(jnp.mean(inputs * inputs, axis=1, keepdims=True) + EPS)
    normed = (inputs * first_scale * gain_one).astype(jnp.bfloat16)
    query_projected = jnp.dot(normed, full_query, preferred_element_type=jnp.float32)
    key_projected = jnp.dot(normed, full_key, preferred_element_type=jnp.float32)
    value_projected = jnp.dot(normed, full_value, preferred_element_type=jnp.float32)
    query_rows = (
        rotary_apply(
            query_projected.reshape(group_count, QUERY_HEADS, HEAD_SIZE), cosine_table, sine_table
        )
        .astype(jnp.bfloat16)
        .reshape(group_count, KEY_VALUE_HEADS, head_groups, HEAD_SIZE)
    )
    key_rows = rotary_apply(
        key_projected.reshape(group_count, KEY_VALUE_HEADS, HEAD_SIZE), cosine_table, sine_table
    ).astype(jnp.bfloat16)
    value_rows = value_projected.astype(jnp.bfloat16).reshape(
        group_count, KEY_VALUE_HEADS, HEAD_SIZE
    )
    mixed, logsum = attend(query_rows, key_rows, value_rows, segment, scale)
    hidden_one = inputs + jnp.dot(mixed, full_output, preferred_element_type=jnp.float32)
    second_scale = lax.rsqrt(jnp.mean(hidden_one * hidden_one, axis=1, keepdims=True) + EPS)
    normed_two = (hidden_one * second_scale * gain_two).astype(jnp.bfloat16)
    picks = expert_ids.shape[1]
    local_experts = gate_weight.shape[0]
    experts = local_experts * shards
    capacity = 3 * group_count * picks // (2 * experts)
    hits = (expert_ids[:, :, None] == jnp.arange(experts, dtype=jnp.int32)[None, None, :]).astype(
        jnp.int32
    )
    per_token = jnp.sum(hits, axis=1)
    before = jnp.cumsum(per_token, axis=0) - per_token
    slot = jnp.sum(hits * before[:, None, :], axis=2)
    target = (expert_ids * capacity + slot).reshape(-1)
    token_index = jnp.broadcast_to(
        jnp.arange(group_count, dtype=jnp.int32)[:, None], expert_ids.shape
    ).reshape(-1)
    source_row = jnp.full((experts * capacity,), group_count, jnp.int32).at[target].set(token_index)
    slot_gate = jnp.zeros((experts * capacity,), jnp.float32).at[target].set(gates.reshape(-1))
    padded = jnp.concatenate([normed_two, jnp.zeros((1, width), jnp.bfloat16)], axis=0)
    outgoing = padded[source_row]
    incoming = lax.all_to_all(outgoing, "shard", split_axis=0, concat_axis=0, tiled=True)
    incoming_four = incoming.reshape(shards, local_experts, capacity, width)
    gate_act, up_act, inner = expert_forward(incoming_four, gate_weight, up_weight)
    result = jnp.einsum(
        "secf,efd->secd", inner, down_weight, preferred_element_type=jnp.float32
    ).astype(jnp.bfloat16)
    returned = lax.all_to_all(
        result.reshape(-1, width), "shard", split_axis=0, concat_axis=0, tiled=True
    )
    picked = returned[target].reshape(group_count, picks, width).astype(jnp.float32)
    layer_out = hidden_one + jnp.sum(gates[:, :, None] * picked, axis=1)
    slope_pad = jnp.concatenate([slope_low, jnp.zeros((1, width), jnp.bfloat16)], axis=0)
    slot_slopes = (slot_gate[:, None] * slope_pad[source_row].astype(jnp.float32)).astype(
        jnp.bfloat16
    )
    rows_back, slopes_in = (
        lax.all_to_all(outgoing, "shard", split_axis=0, concat_axis=0, tiled=True),
        lax.all_to_all(slot_slopes, "shard", split_axis=0, concat_axis=0, tiled=True),
    )
    rows_four = rows_back.reshape(incoming_four.shape)
    gate_act, up_act, inner = expert_forward(rows_four, gate_weight, up_weight)
    slopes_four = slopes_in.reshape(incoming_four.shape)
    delta_down = jnp.einsum(
        "secf,secd->efd", inner, slopes_four, preferred_element_type=jnp.float32
    )
    inner_slope = jnp.einsum(
        "secd,efd->secf", slopes_four, down_weight, preferred_element_type=jnp.float32
    )
    sigmoid_gate = jax.nn.sigmoid(gate_act)
    up_slope = (inner_slope * gate_act * sigmoid_gate).astype(jnp.bfloat16)
    gate_slope = (
        inner_slope * up_act * sigmoid_gate * (1.0 + gate_act * (1.0 - sigmoid_gate))
    ).astype(jnp.bfloat16)
    delta_gate = jnp.einsum(
        "secd,secf->edf", rows_four, gate_slope, preferred_element_type=jnp.float32
    )
    delta_up = jnp.einsum("secd,secf->edf", rows_four, up_slope, preferred_element_type=jnp.float32)
    row_slopes = jnp.einsum(
        "secf,edf->secd", gate_slope, gate_weight, preferred_element_type=jnp.float32
    )
    row_slopes = row_slopes + jnp.einsum(
        "secf,edf->secd", up_slope, up_weight, preferred_element_type=jnp.float32
    )
    back_rows = lax.all_to_all(
        row_slopes.astype(jnp.bfloat16).reshape(-1, width),
        "shard",
        split_axis=0,
        concat_axis=0,
        tiled=True,
    )
    normed_two_slope = jnp.sum(
        back_rows[target].reshape(group_count, picks, width).astype(jnp.float32), axis=1
    )
    hidden_slope, delta_second = norm_back(hidden_one, second_scale, gain_two, normed_two_slope)
    hidden_slope = slopes + hidden_slope
    attn_slope = hidden_slope.astype(jnp.bfloat16)
    delta_output = jnp.einsum("ta,td->ad", mixed, attn_slope, preferred_element_type=jnp.float32)
    mixed_slope = jnp.einsum(
        "td,ad->ta", attn_slope, full_output, preferred_element_type=jnp.float32
    ).astype(jnp.bfloat16)
    query_slope, key_gradient, value_gradient = attend_back(
        query_rows, key_rows, value_rows, segment, scale, logsum, mixed_slope
    )
    query_back = (
        rotary_inverse(query_slope, cosine_table, sine_table)
        .reshape(group_count, QUERY_HEADS * HEAD_SIZE)
        .astype(jnp.bfloat16)
    )
    key_rotated_back = (
        rotary_inverse(key_gradient, cosine_table, sine_table)
        .reshape(group_count, KEY_VALUE_HEADS * HEAD_SIZE)
        .astype(jnp.bfloat16)
    )
    value_returned = value_gradient.reshape(group_count, KEY_VALUE_HEADS * HEAD_SIZE).astype(
        jnp.bfloat16
    )
    delta_query = jnp.einsum("td,ta->da", normed, query_back, preferred_element_type=jnp.float32)
    delta_key = jnp.einsum(
        "td,ta->da", normed, key_rotated_back, preferred_element_type=jnp.float32
    )
    delta_value = jnp.einsum(
        "td,ta->da", normed, value_returned, preferred_element_type=jnp.float32
    )
    normed_slope = jnp.einsum(
        "ta,da->td", query_back, full_query, preferred_element_type=jnp.float32
    )
    normed_slope = normed_slope + jnp.einsum(
        "ta,da->td", key_rotated_back, full_key, preferred_element_type=jnp.float32
    )
    normed_slope = normed_slope + jnp.einsum(
        "ta,da->td", value_returned, full_value, preferred_element_type=jnp.float32
    )
    input_slope, delta_first = norm_back(inputs, first_scale, gain_one, normed_slope)
    input_slope = hidden_slope + input_slope
    shares = (
        lax.psum_scatter(
            delta_first.astype(jnp.bfloat16), "shard", scatter_dimension=0, tiled=True
        ).astype(jnp.float32),
        lax.psum_scatter(
            delta_query.astype(jnp.bfloat16), "shard", scatter_dimension=0, tiled=True
        ).astype(jnp.float32),
        lax.psum_scatter(
            delta_key.astype(jnp.bfloat16), "shard", scatter_dimension=0, tiled=True
        ).astype(jnp.float32),
        lax.psum_scatter(
            delta_value.astype(jnp.bfloat16), "shard", scatter_dimension=0, tiled=True
        ).astype(jnp.float32),
        lax.psum_scatter(
            delta_output.astype(jnp.bfloat16), "shard", scatter_dimension=0, tiled=True
        ).astype(jnp.float32),
        lax.psum_scatter(
            delta_second.astype(jnp.bfloat16), "shard", scatter_dimension=0, tiled=True
        ).astype(jnp.float32),
    )
    summed = (
        lax.psum(shares[0].astype(jnp.bfloat16), "rep").astype(jnp.float32),
        lax.psum(shares[1].astype(jnp.bfloat16), "rep").astype(jnp.float32),
        lax.psum(shares[2].astype(jnp.bfloat16), "rep").astype(jnp.float32),
        lax.psum(shares[3].astype(jnp.bfloat16), "rep").astype(jnp.float32),
        lax.psum(shares[4].astype(jnp.bfloat16), "rep").astype(jnp.float32),
        lax.psum(shares[5].astype(jnp.bfloat16), "rep").astype(jnp.float32),
        lax.psum(delta_gate.astype(jnp.bfloat16), "rep").astype(jnp.float32),
        lax.psum(delta_up.astype(jnp.bfloat16), "rep").astype(jnp.float32),
        lax.psum(delta_down.astype(jnp.bfloat16), "rep").astype(jnp.float32),
    )
    out_rows = layer_out.astype(jnp.bfloat16)[unpack_order]
    slope_rows = input_slope.astype(jnp.bfloat16)[unpack_order]
    out_tokens, delta_tokens = (
        lax.all_to_all(out_rows, "shard", split_axis=0, concat_axis=0, tiled=True),
        lax.all_to_all(slope_rows, "shard", split_axis=0, concat_axis=0, tiled=True),
    )
    return (
        out_tokens,
        delta_tokens,
        summed[0],
        summed[1],
        summed[2],
        summed[3],
        summed[4],
        summed[5],
        summed[6],
        summed[7],
        summed[8],
    )


def solution(mesh):
    placed = (
        P(("rep", "shard"), None),
        P(("rep", "shard"), None),
        P(("rep", "shard"), None),
        P(("rep", "shard")),
        P(("rep", "shard")),
        P(("rep", "shard"), None),
        P(("rep", "shard"), None),
        P("shard"),
        P("shard", None),
        P("shard", None),
        P("shard", None),
        P("shard", None),
        P("shard"),
        P("shard", None, None),
        P("shard", None, None),
        P("shard", None, None),
    )
    return jax.shard_map(
        local,
        mesh=mesh,
        in_specs=placed,
        out_specs=(
            P(("rep", "shard"), None),
            P(("rep", "shard"), None),
            P("shard"),
            P("shard", None),
            P("shard", None),
            P("shard", None),
            P("shard", None),
            P("shard"),
            P("shard", None, None),
            P("shard", None, None),
            P("shard", None, None),
        ),
        check_vma=False,
    )
```

profile of v0, /device:TPU:0, one launch (start us, length us, event | category | flops | bytes accessed | tf_op | source)
XLA Modules:
  0.0 1289.1 jit_solution(15571290540605345703)
XLA Ops:
  17.5 16.9 %all-gather = bf16[8,1,128]{2,1,0:T(2,128)(2,1)S(1)} all-gather(bf16[1,1,128]{2,1,0:T(2,128)(2,1)S(1)} %bitcast.263), channel_id=1, replica_groups=mesh['rep'=4,'shard'=8] {'shard'}, dimensions={0}, use_global_device_ids=true | all-gather | bytes 2304 | tf_op jit(solution)/shard_map/all_gather | solution.py:184
  42.4 15.5 %scatter_custom_fusion = s32[6144]{0:T(1024)S(1)} fusion(s32[4096]{0:T(1024)S(1)} %bitcast.252, s32[4096]{0:T(1024)S(1)} %reshape.362, s32[]{:T(128)} %constant.52.clone.1), kind=kCustom, calls=%fused_computation.139 | custom fusion | bytes 24580 | tf_op jit(solution)/shard_map/scatter | solution.py:234
  75.6 21.3 %all-gather.11.cloned.1.call-done = bf16[1024,1024]{1,0:T(8,128)(2,1)} async-done(((bf16[128,1024]{1,0:T(8,128)(2,1)}), bf16[1024,1024]{1,0:T(8,128)(2,1)}) %all-gather.11.cloned.1.call-update) | async-done | bytes 2097168 | tf_op jit(solution)/shard_map/all_gather | solution.py:185
  117.3 8.5 fusion.57
  131.8 27.3 %gather_fusion.1 = bf16[6144,1024]{1,0:T(8,128)(2,1)} fusion(bf16[513,1024]{1,0:T(8,128)(2,1)S(1)} %concatenate.31, s32[6144]{0:T(1024)S(1)} %copy-done.41), kind=kCustom, calls=%fused_computation.1 | custom fusion | bytes 25190400 | tf_op jit(solution)/shard_map/gather | solution.py:237
  165.0 15.7 %scatter_custom_fusion.1 = f32[6144]{0:T(1024)S(1)} fusion(s32[4096]{0:T(1024)} %bitcast.253, f32[4096]{0:T(1024)S(1)} %reshape.370, f32[]{:T(128)} %constant.53.clone.1), kind=kCustom, calls=%fused_computation.137 | custom fusion | bytes 25088 | tf_op jit(solution)/shard_map/scatter | solution.py:235
  186.9 26.8 %gather_fusion.5 = bf16[6144,1024]{1,0:T(8,128)(2,1)} fusion(bf16[513,1024]{1,0:T(8,128)(2,1)S(1)} %concatenate.32, s32[6144]{0:T(1024)S(1)} %copy-done.41), kind=kCustom, calls=%fused_computation.5 | custom fusion | bytes 25190400 | tf_op jit(solution)/shard_map/gather | solution.py:250
  213.6 11.1 fusion
  224.8 79.0 %all-to-all-done.1 = bf16[8,768,1024]{2,1,0:T(8,128)(2,1)} async-done(((bf16[8,768,1024]{2,1,0:T(8,128)(2,1)}), bf16[8,768,1024]{2,1,0:T(8,128)(2,1)}, u32[]{:S(2)}, u32[]{:S(2)}) %all-to-all-start.1) | async-done | bytes 12582944 | tf_op jit(solution)/shard_map/all_to_all | solution.py:238
  309.1 14.5 %fusion.22 = f32[2,8,384,512]{3,2,1,0:T(8,128)} fusion(bf16[8,2,384,1024]{3,2,1,0:T(8,128)(2,1)} %bitcast.26, bf16[2,1024,512]{2,1,0:T(8,128)(2,1)} %param.30), kind=kOutput, calls=%fused_computation.49 | convolution fusion | flops 6442450944 | bytes 27262976 | tf_op jit(solution)/shard_map/secd,edf->secf/dot_general | solution.py:149
  323.5 14.5 %fusion.24 = f32[2,8,384,512]{3,2,1,0:T(8,128)} fusion(bf16[8,2,384,1024]{3,2,1,0:T(8,128)(2,1)} %bitcast.26, bf16[2,1024,512]{2,1,0:T(8,128)(2,1)} %param.29), kind=kOutput, calls=%fused_computation.51 | convolution fusion | flops 6442450944 | bytes 27262976 | tf_op jit(solution)/shard_map/secd,edf->secf/dot_general | solution.py:148
  338.0 110.0 %all-to-all-done.5 = bf16[8,768,1024]{2,1,0:T(8,128)(2,1)} async-done(((bf16[8,768,1024]{2,1,0:T(8,128)(2,1)}), bf16[8,768,1024]{2,1,0:T(8,128)(2,1)}, u32[]{:S(2)}, u32[]{:S(2)}) %all-to-all-start.5) | async-done | bytes 12582944 | tf_op jit(solution)/shard_map/all_to_all | solution.py:255
  448.1 23.8 %fusion.12 = (bf16[8,2,384,512]{3,2,0,1:T(8,128)(2,1)}, bf16[8,2,384,512]{3,2,0,1:T(8,128)(2,1)}, bf16[8,2,384,512]{3,2,0,1:T(8,128)(2,1)}) fusion(f32[2,8,384,512]{3,2,1,0:T(8,128)} %fusion.24, f32[2,8,384,512]{3,2,1,0:T(8,128)} %fusion.22, bf16[2,512,1024]{2,1,0:T(8,128)(2,1)S(1)} %copy-done, bf16[8,2,384,1024]{3,2,1,0:T(8,128)(2,1)} %bitcast.44), kind=kOutput, calls=%fused_computation.34 | convolution fusion | flops 6492782592 | bytes 58720256 | tf_op jit(solution)/shard_map/secd,efd->secf/dot_general | solution.py:263
  471.9 9.8 convert_bitcast_fusion
  492.7 14.6 %fusion.52 = f32[2,8,384,1024]{3,2,1,0:T(8,128)} fusion(bf16[8,2,384,512]{3,2,0,1:T(8,128)(2,1)} %get-tuple-element.80, bf16[2,1024,512]{2,1,0:T(8,128)(2,1)S(1)} %copy-done.64), kind=kOutput, calls=%fused_computation.81 | convolution fusion | flops 6442450944 | bytes 33554432 | tf_op jit(solution)/shard_map/secf,edf->secd/dot_general | solution.py:275
  507.3 17.4 %fusion.7 = bf16[8,2,384,1024]{3,2,0,1:T(8,128)(2,1)} fusion(f32[2,8,384,1024]{3,2,1,0:T(8,128)} %fusion.52, bf16[8,2,384,512]{3,2,0,1:T(8,128)(2,1)} %get-tuple-element.79, bf16[2,1024,512]{2,1,0:T(8,128)(2,1)} %param.30), kind=kOutput, calls=%fused_computation.27 | convolution fusion | flops 6455033856 | bytes 46137344 | tf_op jit(solution)/shard_map/secf,edf->secd/dot_general | solution.py:278
  524.7 10.6 copy.101
  535.3 96.4 %all-to-all-done.2 = bf16[8,768,1024]{2,1,0:T(8,128)(2,1)} async-done(((bf16[8,768,1024]{2,1,0:T(8,128)(2,1)}), bf16[8,768,1024]{2,1,0:T(8,128)(2,1)}, u32[]{:S(2)}, u32[]{:S(2)}) %all-to-all-start.2) | async-done | bytes 12582944 | tf_op jit(solution)/shard_map/all_to_all | solution.py:244
  637.3 27.2 %gather_fusion.2 = bf16[4096,1024]{1,0:T(8,128)(2,1)} fusion(bf16[6144,1024]{1,0:T(8,128)(2,1)} %bitcast.37, s32[4096]{0:T(1024)S(1)} %broadcast_clamp_fusion), kind=kCustom, calls=%fused_computation.2 | custom fusion | bytes 16793600 | tf_op jit(solution)/shard_map/gather | solution.py:247
  664.5 111.7 %all-to-all-done.6 = bf16[8,768,1024]{2,1,0:T(8,128)(2,1)} async-done(((bf16[8,768,1024]{2,1,0:T(8,128)(2,1)}), bf16[8,768,1024]{2,1,0:T(8,128)(2,1)}, u32[]{:S(2)}, u32[]{:S(2)}) %all-to-all-start.6) | async-done | bytes 12582944 | tf_op jit(solution)/shard_map/all_to_all | solution.py:281
  776.2 27.1 %gather_fusion.6 = bf16[4096,1024]{1,0:T(8,128)(2,1)} fusion(bf16[6144,1024]{1,0:T(8,128)(2,1)} %bitcast.51, s32[4096]{0:T(1024)S(1)} %broadcast_clamp_fusion), kind=kCustom, calls=%fused_computation.6 | custom fusion | bytes 16793600 | tf_op jit(solution)/shard_map/gather | solution.py:289
  803.2 15.7 %convert_reduce_fusion = (f32[512,1024]{1,0:T(8,128)S(1)}, f32[512,1024]{1,0:T(8,128)S(1)}) fusion(bf16[4096,1024]{1,0:T(8,128)(2,1)} %gather_fusion.6, bf16[4096,1024]{1,0:T(8,128)(2,1)} %gather_fusion.2, f32[512,8]{1,0:T(8,128)S(1)} %copy-done.13), kind=kLoop, calls=%fused_computation.13 | loop fusion | flops 19922944 | bytes 20987904 | tf_op jit(solution)/shard_map/reduce_sum | solution.py:288
  832.6 11.3 fusion.2
  845.9 12.9 fusion.4
  879.6 13.8 %bitcast_convert_fusion = bf16[2,512,1024]{2,1,0:T(8,128)(2,1)} fusion(bf16[8,2,384,512]{3,2,0,1:T(8,128)(2,1)} %get-tuple-element.81, bf16[8,2,384,1024]{3,2,1,0:T(8,128)(2,1)} %bitcast.44), kind=kOutput, calls=%fused_computation.66 | convolution fusion | flops 6443499520 | bytes 20971520 | tf_op jit(solution)/shard_map/secf,secd->efd/dot_general | solution.py:260
  893.4 12.9 %bitcast_convert_fusion.1 = bf16[2,1024,512]{2,1,0:T(8,128)(2,1)} fusion(bf16[8,2,384,1024]{3,2,1,0:T(8,128)(2,1)} %bitcast.26, bf16[8,2,384,512]{3,2,0,1:T(8,128)(2,1)} %get-tuple-element.79), kind=kOutput, calls=%fused_computation.67 | convolution fusion | flops 6443499520 | bytes 20971520 | tf_op jit(solution)/shard_map/secd,secf->edf/dot_general | solution.py:274
  906.3 10.7 bitcast_convert_fusion.2
  920.8 45.1 %reduce-scatter.11.cloned.1.call-done = bf16[128,1024]{1,0:T(8,128)(2,1)} async-done(((bf16[1024,1024]{1,0:T(8,128)(2,1)}), bf16[128,1024]{1,0:T(8,128)(2,1)}) %reduce-scatter.11.cloned.1.call-update) | async-done | bytes 262160 | tf_op jit(solution)/shard_map/reduce_scatter | solution.py:345
  965.9 45.5 %reduce-scatter.5.cloned.1.call-done = bf16[128,1024]{1,0:T(8,128)(2,1)} async-done(((bf16[1024,1024]{1,0:T(8,128)(2,1)}), bf16[128,1024]{1,0:T(8,128)(2,1)}) %reduce-scatter.5.cloned.1.call-update) | async-done | bytes 262160 | tf_op jit(solution)/shard_map/reduce_scatter | solution.py:336
  1039.0 21.3 %all-reduce.4 = (bf16[1024]{0:T(1024)(128)(2,1)S(1)}, bf16[1024]{0:T(1024)(128)(2,1)S(1)}) all-reduce(bf16[1024]{0:T(1024)(128)(2,1)S(1)} %get-tuple-element.54, bf16[1024]{0:T(1024)(128)(2,1)S(1)} %get-tuple-element.52), channel_id=2, replica_groups=mesh['rep'=4,'shard'=8] {'shard'}, use_global_device_ids=true, to_apply=%region_19.20.clone | all-reduce | flops 2048 | bytes 8192
  1060.5 14.0 %all-reduce.5 = (bf16[128]{0:T(256)(128)(2,1)S(1)}, bf16[128]{0:T(256)(128)(2,1)S(1)}) all-reduce(bf16[128]{0:T(256)(128)(2,1)S(1)} %dynamic-slice.1, bf16[128]{0:T(256)(128)(2,1)S(1)} %dynamic-slice.3), channel_id=1, replica_groups=mesh['rep'=4,'shard'=8] {'rep'}, use_global_device_ids=true, to_apply=%region_20.21 | all-reduce | flops 256 | bytes 1024 | tf_op jit(solution)/shard_map/psum | solution.py:353
  1075.6 189.4 %all-reduce.9.cloned.1.call-done = (bf16[128,1024]{1,0:T(8,128)(2,1)}, bf16[128,512]{1,0:T(8,128)(2,1)}, bf16[128,512]{1,0:T(8,128)(2,1)}, bf16[128,1024]{1,0:T(...) async-done(((bf16[128,1024]{1,0:T(8,128)(2,1)}, bf16[128,512]{1,0:T(8,128)(2,1)}, ...) | async-done | bytes 7077904 | tf_op jit(solution)/shard_map/psum | solution.py:354
  (264 shorter events, 181.1 us)
Async XLA Ops:
  7.2 440.9 %copy-start = (bf16[2,512,1024]{2,1,0:T(8,128)(2,1)S(1)}, bf16[2,512,1024]{2,1,0:T(8,128)(2,1)}, u32[]{:S(2)}) copy-start(bf16[2,512,1024]{2,1,0:T(8,128)(2,1)} %param.31) | copy-start | bytes 6291460
  7.2 27.2 %copy-start.63 = (bf16[128]{0:T(256)(128)(2,1)S(1)}, bf16[128]{0:T(256)(128)(2,1)}, u32[]{:S(2)}) copy-start(bf16[128]{0:T(256)(128)(2,1)} %param.28) | copy-start | bytes 772
  7.2 62.0 %all-gather.9.cloned.1.call-start = ((), (), s32[]{:S(2)}) async-start(), calls=%async_computation.13 | async-start | bytes 1179648 | tf_op jit(solution)/shard_map/all_gather | solution.py:186
  8.0 64.6 %all-gather.7.cloned.1.call-start = ((), (), s32[]{:S(2)}) async-start(), calls=%async_computation.12 | async-start | bytes 1179648 | tf_op jit(solution)/shard_map/all_gather | solution.py:187
  8.7 88.1 %all-gather.11.cloned.1.call-start = ((), (), s32[]{:S(2)}) async-start(), calls=%async_computation.14 | async-start | bytes 2359296 | tf_op jit(solution)/shard_map/all_gather | solution.py:185
  9.5 50.3 %all-to-all-start = ((bf16[8,64,1024]{2,1,0:T(8,128)(2,1)}), bf16[8,64,1024]{2,1,0:T(8,128)(2,1)S(1)}, u32[]{:S(2)}, u32[]{:S(2)}) async-start(bf16[8,64,1024]{2,1,0:T(8,128)(2,1)} %bitcast.235), calls=%async_computation | async-start | bytes 2097152 | tf_op jit(solution)/shard_map/all_to_all | solution.py:176
  14.6 111.9 %all-gather.13.cloned.1.call-start = ((), (), s32[]{:S(2)}) async-start(), calls=%async_computation.15 | async-start | bytes 2359296 | tf_op jit(solution)/shard_map/all_gather | solution.py:188
  17.4 49.7 %copy-start.49 = (s32[4096,1]{0,1:T(1,128)}, s32[4096,1]{0,1:T(1,128)S(1)}, u32[]{:S(2)}) copy-start(s32[4096,1]{0,1:T(1,128)S(1)} %compare_select_fusion) | copy-start | bytes 49156
  34.4 62.4 %copy-start.51 = (f32[8,1,128]{2,1,0:T(1,128)}, f32[8,1,128]{2,1,0:T(1,128)S(1)}, u32[]{:S(2)}) copy-start(f32[8,1,128]{2,1,0:T(1,128)S(1)} %convert_element_type.252) | copy-start | bytes 12292
  42.2 88.2 %copy-start.47 = (f32[8,1,128]{2,1,0:T(1,128)}, f32[8,1,128]{2,1,0:T(1,128)S(1)}, u32[]{:S(2)}) copy-start(f32[8,1,128]{2,1,0:T(1,128)S(1)} %convert_element_type.253) | copy-start | bytes 12292
  58.9 41.0 %copy-start.26 = (f32[512,32]{0,1:T(8,128)}, f32[512,32]{0,1:T(8,128)S(1)}, u32[]{:S(2)}) copy-start(f32[512,32]{0,1:T(8,128)S(1)} %get-tuple-element.92) | copy-start | bytes 196612
  58.9 41.0 %copy-start.28 = (f32[512,32]{0,1:T(8,128)}, f32[512,32]{0,1:T(8,128)S(1)}, u32[]{:S(2)}) copy-start(f32[512,32]{0,1:T(8,128)S(1)} %get-tuple-element.93) | copy-start | bytes 196612
  59.8 99.4 %all-to-all-start.4 = ((bf16[8,64,1024]{2,1,0:T(8,128)(2,1)}), bf16[8,64,1024]{2,1,0:T(8,128)(2,1)}, u32[]{:S(2)}, u32[]{:S(2)}) async-start(bf16[8,64,1024]{2,1,0:T(8,128)(2,1)} %bitcast.236), calls=%async_computation.4 | async-start | bytes 2097152 | tf_op jit(solution)/shard_map/all_to_all | solution.py:177
  69.2 27.6 %copy-start.55 = (f32[512]{0:T(512)}, f32[512]{0:T(512)S(1)}, u32[]{:S(2)}) copy-start(f32[512]{0:T(512)S(1)} %get-tuple-element.95) | copy-start | bytes 6148
  72.6 27.7 %copy-start.32 = (bf16[512,8,32]{0,2,1:T(8,128)(2,1)}, bf16[512,8,32]{0,2,1:T(8,128)(2,1)S(1)}, u32[]{:S(2)}) copy-start(bf16[512,8,32]{0,2,1:T(8,128)(2,1)S(1)} %get-tuple-element.90) | copy-start | bytes 786436
  159.2 144.5 %all-to-all-start.1 = ((bf16[8,768,1024]{2,1,0:T(8,128)(2,1)}), bf16[8,768,1024]{2,1,0:T(8,128)(2,1)}, u32[]{:S(2)}, u32[]{:S(2)}) async-start(bf16[8,768,1024]{2,1,0:T(8,128)(2,1)} %bitcast.219), calls=%async_computation.1 | async-start | bytes 25165824 | tf_op jit(solution)/shard_map/all_to_all | solution.py:238
  164.9 15.9 %copy-start.12 = (f32[512,8]{1,0:T(8,128)}, f32[512,8]{1,0:T(8,128)S(1)}, u32[]{:S(2)}) copy-start(f32[512,8]{1,0:T(8,128)S(1)} %copy.92) | copy-start | bytes 49156
  303.7 144.3 %all-to-all-start.5 = ((bf16[8,768,1024]{2,1,0:T(8,128)(2,1)}), bf16[8,768,1024]{2,1,0:T(8,128)(2,1)}, u32[]{:S(2)}, u32[]{:S(2)}) async-start(bf16[8,768,1024]{2,1,0:T(8,128)(2,1)} %fusion), calls=%async_computation.5 | async-start | bytes 25165824 | tf_op jit(solution)/shard_map/all_to_all | solution.py:255
  487.1 144.5 %all-to-all-start.2 = ((bf16[8,768,1024]{2,1,0:T(8,128)(2,1)}), bf16[8,768,1024]{2,1,0:T(8,128)(2,1)}, u32[]{:S(2)}, u32[]{:S(2)}) async-start(bf16[8,768,1024]{2,1,0:T(8,128)(2,1)} %bitcast.218), calls=%async_computation.2 | async-start | bytes 25165824 | tf_op jit(solution)/shard_map/all_to_all | solution.py:244
  631.7 144.5 %all-to-all-start.6 = ((bf16[8,768,1024]{2,1,0:T(8,128)(2,1)}), bf16[8,768,1024]{2,1,0:T(8,128)(2,1)}, u32[]{:S(2)}, u32[]{:S(2)}) async-start(bf16[8,768,1024]{2,1,0:T(8,128)(2,1)} %bitcast.217), calls=%async_computation.6 | async-start | bytes 25165824 | tf_op jit(solution)/shard_map/all_to_all | solution.py:281
  637.1 279.8 %reduce-scatter.9.cloned.1.call-start = ((), (), s32[]{:S(2)}) async-start(), calls=%async_computation.18 | async-start | bytes 1179648 | tf_op jit(solution)/shard_map/reduce_scatter | solution.py:342
  776.2 27.1 %copy-start.13 = (f32[512,8]{1,0:T(8,128)S(1)}, f32[512,8]{1,0:T(8,128)}, u32[]{:S(2)}) copy-start(f32[512,8]{1,0:T(8,128)} %copy-done.12) | copy-start | bytes 49156
  803.2 15.7 %copy-start.48 = (f32[8,1,128]{2,1,0:T(1,128)S(1)}, f32[8,1,128]{2,1,0:T(1,128)}, u32[]{:S(2)}) copy-start(f32[8,1,128]{2,1,0:T(1,128)} %copy-done.47) | copy-start | bytes 12292
  803.2 15.7 %copy-start.54 = (f32[512]{0:T(512)S(1)}, f32[512]{0:T(512)}, u32[]{:S(2)}) copy-start(f32[512]{0:T(512)} %copy-done.53) | copy-start | bytes 6148
  845.9 75.0 %reduce-scatter.7.cloned.1.call-start = ((), (), s32[]{:S(2)}) async-start(), calls=%async_computation.17 | async-start | bytes 1179648 | tf_op jit(solution)/shard_map/reduce_scatter | solution.py:339
  865.1 100.9 %reduce-scatter.11.cloned.1.call-start = ((), (), s32[]{:S(2)}) async-start(), calls=%async_computation.19 | async-start | bytes 2359296 | tf_op jit(solution)/shard_map/reduce_scatter | solution.py:345
  869.3 142.1 %reduce-scatter.5.cloned.1.call-start = ((), (), s32[]{:S(2)}) async-start(), calls=%async_computation.16 | async-start | bytes 2359296 | tf_op jit(solution)/shard_map/reduce_scatter | solution.py:336
  879.5 385.5 %all-reduce.9.cloned.1.call-start = ((), (), s32[]{:S(2)}) async-start(), calls=%async_computation.20 | async-start | bytes 14155776 | tf_op jit(solution)/shard_map/psum | solution.py:354
  879.6 26.7 %slice-start = ((s8[6291456]{0:T(1024)(128)(4,1)}), s8[4194304]{0:T(1024)(128)(4,1)S(1)}, s32[]{:S(2)}) async-start(s8[6291456]{0:T(1024)(128)(4,1)} %bitcast.267), calls=%async_computation.21 | async-start | bytes 8388608
  1014.9 19.3 %all-to-all-start.3 = ((bf16[8,64,1024]{2,1,0:T(8,128)(2,1)}), bf16[8,64,1024]{2,1,0:T(8,128)(2,1)S(1)}, u32[]{:S(2)}, u32[]{:S(2)}) async-start(bf16[8,64,1024]{2,1,0:T(8,128)(2,1)} %bitcast.39), calls=%async_computation.3 | async-start | bytes 2097152 | tf_op jit(solution)/shard_map/all_to_all | solution.py:366
  1034.2 41.4 %all-to-all-start.7 = ((bf16[8,64,1024]{2,1,0:T(8,128)(2,1)}), bf16[8,64,1024]{2,1,0:T(8,128)(2,1)S(1)}, u32[]{:S(2)}, u32[]{:S(2)}) async-start(bf16[8,64,1024]{2,1,0:T(8,128)(2,1)} %bitcast.70), calls=%async_computation.7 | async-start | bytes 2097152 | tf_op jit(solution)/shard_map/all_to_all | solution.py:367
  1075.6 199.0 %copy-start.10 = (bf16[8,64,1024]{2,1,0:T(8,128)(2,1)}, bf16[8,64,1024]{2,1,0:T(8,128)(2,1)S(1)}, u32[]{:S(2)}) copy-start(bf16[8,64,1024]{2,1,0:T(8,128)(2,1)S(1)} %all-to-all-done.7) | copy-start | bytes 3145732
  (55 other events, 278.8 us)
Sparse Core Ops, SparseCore 0:
  10.0 30.4 all-gather.8
  42.4 23.5 all-gather.6
  67.9 28.9 all-gather.10
  98.6 27.8 all-gather.12
  846.0 35.1 reduce-scatter.8
  884.8 36.0 reduce-scatter.6
  924.7 41.1 reduce-scatter.10
  970.1 41.2 reduce-scatter.4
  1014.4 250.5 all-reduce.8
where the time goes:
time: 1290 us
  waiting for transfers between devices  711 us (55%)
  matrix products  204 us (16%)
  local copies, waits for them, and re-layouts  185 us (14%)
  other arithmetic  73.9 us (6%)
  blocking collectives  60 us (5%)
  starting transfers between devices  39.4 us (3%)
  between operations  15.7 us (1%)
    psum x1, waiting for transfers between devices, local(): lax.psum(shares[1].astype(jnp.bfloat16), 'rep').astype(jnp.float32)  189 us
    all_to_all x1, waiting for transfers between devices, local(): lax.all_to_all(row_slopes.astype(jnp.bfloat16).reshape(-1, width), 'shard...  112 us
    all_to_all x1, waiting for transfers between devices, local(): lax.all_to_all(slot_slopes, 'shard', split_axis=0, concat_axis=0, tiled=T...  110 us
    all_to_all x1, waiting for transfers between devices, local(): lax.all_to_all(result.reshape(-1, width), 'shard', split_axis=0, concat_a...  96.4 us
    all_to_all x1, waiting for transfers between devices, local(): lax.all_to_all(outgoing, 'shard', split_axis=0, concat_axis=0, tiled=True)  79 us
    reduce_scatter x1, waiting for transfers between devices, local(): lax.psum_scatter(delta_query.astype(jnp.bfloat16), 'shard', scatter_dimen...  45.5 us
    reduce_scatter x1, waiting for transfers between devices, local(): lax.psum_scatter(delta_output.astype(jnp.bfloat16), 'shard', scatter_dime...  45.1 us
    gather x1, local copies, waits for them, and re-layouts, local(): outgoing = padded[source_row]  27.3 us
  transfers between devices with their start and end apart: 17, of which 11 were waited for; matrix products, arithmetic and copies ran while one was open for 26% of the time, Pallas kernels for 0%

commit v1 on v0

v1 whole, which is shorter than its diff:
```python
import jax
import jax.numpy as jnp
from jax import lax
from jax.sharding import PartitionSpec as P

QUERY_HEADS = 16
KEY_VALUE_HEADS = 8
HEAD_SIZE = 64


EPS = 1e-05
THETA = 10000.0


def rope_tables(place, size):
    half = size // 2
    freq = THETA ** (-2.0 * jnp.arange(half, dtype=jnp.float32) / size)
    angle = place.astype(jnp.float32)[:, None] * freq[None, :]
    return (jnp.cos(angle), jnp.sin(angle))


def rotary_apply(heads, cosine_table, sine_table):
    half = heads.shape[-1] // 2
    first = heads[..., :half]
    second = heads[..., half:]
    along = cosine_table[:, None, :]
    across = sine_table[:, None, :]
    return jnp.concatenate(
        [first * along - second * across, second * along + first * across], axis=-1
    )


def rotary_inverse(heads, cosine_table, sine_table):
    half = heads.shape[-1] // 2
    first = heads[..., :half]
    second = heads[..., half:]
    along = cosine_table[:, None, :]
    across = sine_table[:, None, :]
    return jnp.concatenate(
        [first * along + second * across, second * along - first * across], axis=-1
    )


def segment_info(lengths, group_count):
    ends = jnp.cumsum(lengths)
    starts = ends - lengths
    place = jnp.arange(group_count, dtype=jnp.int32)
    inside = ((place[:, None] >= starts[None, :]) & (place[:, None] < ends[None, :])).astype(
        jnp.int32
    )
    segment = jnp.sum(inside * jnp.arange(lengths.shape[0], dtype=jnp.int32)[None, :], axis=1)
    offset = jnp.sum(inside * starts[None, :], axis=1)
    return (segment, place - offset)


def masked_scores(query_block, key_rows, start, segment, scale):
    width = query_block.shape[0]
    scores = (
        jnp.einsum("igzd,jgd->gzij", query_block, key_rows, preferred_element_type=jnp.float32)
        * scale
    )
    rows = start + jnp.arange(width, dtype=jnp.int32)
    columns = jnp.arange(key_rows.shape[0], dtype=jnp.int32)
    allowed = (segment[:, None] == segment[None, :]) & (columns[None, :] <= rows[:, None])
    return jnp.where(allowed, scores, -1e30)


def block_starts(group_count):
    width = min(512, group_count)
    blocks = group_count // width
    return (width, blocks, jnp.arange(blocks, dtype=jnp.int32) * width)


def attend(query_rows, key_rows, value_rows, segment, scale):
    group_count = query_rows.shape[0]
    width, blocks, starts = block_starts(group_count)
    grouped = query_rows.reshape((blocks, width) + query_rows.shape[1:])

    def one_block(piece):
        query_block, start = piece
        scores = masked_scores(query_block, key_rows, start, segment, scale)
        largest = jnp.max(scores, axis=-1, keepdims=True)
        powers = jnp.exp(scores - largest)
        totals = jnp.sum(powers, axis=-1, keepdims=True)
        weights = (powers / totals).astype(jnp.bfloat16)
        mixed = jnp.einsum(
            "gzij,jgd->igzd", weights, value_rows, preferred_element_type=jnp.float32
        )
        return (mixed.astype(jnp.bfloat16), (largest + jnp.log(totals))[..., 0])

    mixed, logsum = lax.map(one_block, (grouped, starts))
    return (mixed.reshape(group_count, -1), logsum)


def attend_back(query_rows, key_rows, value_rows, segment, scale, logsum, mixed_slope):
    group_count = query_rows.shape[0]
    width, blocks, starts = block_starts(group_count)
    grouped = query_rows.reshape((blocks, width) + query_rows.shape[1:])
    slope_blocks = mixed_slope.reshape(grouped.shape)

    def one_block(piece):
        query_block, slope_block, logsum_block, start = piece
        scores = masked_scores(query_block, key_rows, start, segment, scale)
        probs = jnp.exp(scores - logsum_block[..., None])
        prob_slope = jnp.einsum(
            "igzd,jgd->gzij", slope_block, value_rows, preferred_element_type=jnp.float32
        )
        inner = jnp.sum(probs * prob_slope, axis=-1, keepdims=True)
        score_slope = (probs * (prob_slope - inner)).astype(jnp.bfloat16)
        query_slope = (
            jnp.einsum("gzij,jgd->igzd", score_slope, key_rows, preferred_element_type=jnp.float32)
            * scale
        )
        key_gradient = (
            jnp.einsum(
                "gzij,igzd->jgd", score_slope, query_block, preferred_element_type=jnp.float32
            )
            * scale
        )
        value_gradient = jnp.einsum(
            "gzij,igzd->jgd",
            probs.astype(jnp.bfloat16),
            slope_block,
            preferred_element_type=jnp.float32,
        )
        return (query_slope, key_gradient, value_gradient)

    query_slope, key_gradient, value_gradient = lax.map(
        one_block, (grouped, slope_blocks, logsum, starts)
    )
    return (
        query_slope.reshape(group_count, -1, query_rows.shape[-1]),
        jnp.sum(key_gradient, axis=0),
        jnp.sum(value_gradient, axis=0),
    )


def norm_back(inputs, scale_rows, gain, slope):
    scaled = slope * gain
    gain_slope = jnp.sum(slope * inputs * scale_rows, axis=0)
    input_slope = scale_rows * scaled - inputs * scale_rows**3 * jnp.mean(
        inputs * scaled, axis=1, keepdims=True
    )
    return (input_slope, gain_slope)


def local(
    tokens,
    cotangent,
    seq_lengths,
    pack_order,
    unpack_order,
    expert_ids,
    gates,
    first_gain,
    query_weight,
    key_matrix,
    value_matrix,
    output_weight,
    second_gain,
    gate_weight,
    up_weight,
    down_weight,
):
    shards = lax.axis_size("shard")
    me = lax.axis_index("shard")
    group_count, width = tokens.shape
    block = group_count // shards
    low = jnp.bfloat16
    full = jnp.float32
    arrived = lax.all_to_all(tokens, "shard", split_axis=0, concat_axis=0, tiled=True)
    inputs_low = arrived[pack_order]
    inputs = inputs_low.astype(full)
    query_width = query_weight.shape[1]
    key_width = key_matrix.shape[1]
    joined = lax.all_gather(
        jnp.concatenate([query_weight, key_matrix, value_matrix, output_weight], axis=1),
        "shard",
        axis=0,
        tiled=True,
    )
    full_query = joined[:, :query_width]
    full_key = joined[:, query_width : query_width + key_width]
    full_value = joined[:, query_width + key_width : query_width + 2 * key_width]
    full_output = joined[:, query_width + 2 * key_width :]
    gains = lax.all_gather(jnp.stack([first_gain, second_gain]), "shard", axis=1, tiled=True)
    gain_one = gains[0].astype(full)
    gain_two = gains[1].astype(full)
    all_slopes = lax.all_gather(cotangent, "shard", axis=0, tiled=False)
    slope_arrived = lax.dynamic_slice_in_dim(all_slopes, me * block, block, axis=1).reshape(
        group_count, width
    )
    slope_low = slope_arrived[pack_order]
    slopes = slope_low.astype(full)
    segment, place = segment_info(seq_lengths[0], group_count)
    cosine_table, sine_table = rope_tables(place, HEAD_SIZE)
    scale = HEAD_SIZE ** (-0.5)
    head_groups = QUERY_HEADS // KEY_VALUE_HEADS
    first_scale = lax.rsqrt(jnp.mean(inputs * inputs, axis=1, keepdims=True) + EPS)
    normed = (inputs * first_scale * gain_one).astype(low)
    query_projected = jnp.dot(normed, full_query, preferred_element_type=full)
    key_projected = jnp.dot(normed, full_key, preferred_element_type=full)
    value_projected = jnp.dot(normed, full_value, preferred_element_type=full)
    query_rows = (
        rotary_apply(
            query_projected.reshape(group_count, QUERY_HEADS, HEAD_SIZE), cosine_table, sine_table
        )
        .astype(low)
        .reshape(group_count, KEY_VALUE_HEADS, head_groups, HEAD_SIZE)
    )
    key_rows = rotary_apply(
        key_projected.reshape(group_count, KEY_VALUE_HEADS, HEAD_SIZE), cosine_table, sine_table
    ).astype(low)
    value_rows = value_projected.astype(low).reshape(group_count, KEY_VALUE_HEADS, HEAD_SIZE)
    mixed, logsum = attend(query_rows, key_rows, value_rows, segment, scale)
    hidden_one = inputs + jnp.dot(mixed, full_output, preferred_element_type=full)
    second_scale = lax.rsqrt(jnp.mean(hidden_one * hidden_one, axis=1, keepdims=True) + EPS)
    normed_two = (hidden_one * second_scale * gain_two).astype(low)
    local_experts = gate_weight.shape[0]
    experts = local_experts * shards
    hidden_width = gate_weight.shape[2]
    hits = expert_ids[:, :, None] == jnp.arange(experts, dtype=jnp.int32)[None, None, :]
    mixing = jnp.sum(jnp.where(hits, gates[:, :, None], 0.0), axis=1)[unpack_order]
    mixing = lax.all_to_all(mixing.T, "shard", split_axis=0, concat_axis=0, tiled=True)
    mixing = mixing.reshape(shards, local_experts, shards, block)
    mixing = mixing.transpose(1, 2, 0, 3).reshape(local_experts, shards * group_count, 1)

    def swap(rows):
        return rows.reshape(shards, shards, block, width).swapaxes(0, 1).reshape(-1, width)

    rows = swap(lax.all_gather(normed_two[unpack_order], "shard", axis=0, tiled=True))
    slope_rows = all_slopes.reshape(-1, width)
    gate_act = jnp.einsum("td,edf->etf", rows, gate_weight, preferred_element_type=full)
    up_act = jnp.einsum("td,edf->etf", rows, up_weight, preferred_element_type=full)
    sigmoid_gate = jax.nn.sigmoid(gate_act)
    silu_gate = gate_act * sigmoid_gate
    inner = (mixing * (silu_gate * up_act)).astype(low)
    inner_slope = mixing * jnp.einsum(
        "td,efd->etf", slope_rows, down_weight, preferred_element_type=full
    )
    up_slope = (inner_slope * silu_gate).astype(low)
    gate_slope = (
        inner_slope * up_act * sigmoid_gate * (1.0 + gate_act * (1.0 - sigmoid_gate))
    ).astype(low)
    delta_down = jnp.einsum("etf,td->efd", inner, slope_rows, preferred_element_type=full)
    delta_gate = jnp.einsum("td,etf->edf", rows, gate_slope, preferred_element_type=full)
    delta_up = jnp.einsum("td,etf->edf", rows, up_slope, preferred_element_type=full)
    expert_deltas = lax.psum(
        (delta_gate.astype(low), delta_up.astype(low), delta_down.astype(low)), "rep"
    )
    row_slopes = jnp.einsum("etf,edf->td", gate_slope, gate_weight, preferred_element_type=full)
    row_slopes = row_slopes + jnp.einsum(
        "etf,edf->td", up_slope, up_weight, preferred_element_type=full
    )
    back = lax.psum_scatter(
        swap(row_slopes.astype(low)), "shard", scatter_dimension=0, tiled=True
    )
    normed_two_slope = back[pack_order].astype(full)
    result = jnp.einsum("etf,efd->td", inner, down_weight, preferred_element_type=full)
    shared = lax.dynamic_update_slice_in_dim(
        jnp.zeros((shards, shards, block, width), low),
        hidden_one.astype(low)[unpack_order].reshape(shards, 1, block, width),
        me,
        axis=1,
    ).reshape(-1, width)
    out_tokens = lax.psum_scatter(
        (result + shared.astype(full)).astype(low), "shard", scatter_dimension=0, tiled=True
    )
    hidden_slope, delta_second = norm_back(hidden_one, second_scale, gain_two, normed_two_slope)
    hidden_slope = slopes + hidden_slope
    attn_slope = hidden_slope.astype(low)
    delta_output = jnp.einsum("ta,td->ad", mixed, attn_slope, preferred_element_type=full)
    mixed_slope = jnp.einsum(
        "td,ad->ta", attn_slope, full_output, preferred_element_type=full
    ).astype(low)
    query_slope, key_gradient, value_gradient = attend_back(
        query_rows, key_rows, value_rows, segment, scale, logsum, mixed_slope
    )
    query_back = (
        rotary_inverse(query_slope, cosine_table, sine_table)
        .reshape(group_count, QUERY_HEADS * HEAD_SIZE)
        .astype(low)
    )
    key_back = (
        rotary_inverse(key_gradient, cosine_table, sine_table)
        .reshape(group_count, KEY_VALUE_HEADS * HEAD_SIZE)
        .astype(low)
    )
    value_back = value_gradient.reshape(group_count, KEY_VALUE_HEADS * HEAD_SIZE).astype(low)
    backs = jnp.concatenate([query_back, key_back, value_back], axis=1)
    inputs_width = backs.shape[1]
    deltas = jnp.einsum("td,ta->da", normed, backs, preferred_element_type=full)
    normed_slope = jnp.einsum(
        "ta,da->td", backs, joined[:, :inputs_width], preferred_element_type=full
    )
    input_slope, delta_first = norm_back(inputs, first_scale, gain_one, normed_slope)
    input_slope = (hidden_slope + input_slope).astype(low)
    delta_tokens = lax.all_to_all(
        input_slope[unpack_order], "shard", split_axis=0, concat_axis=0, tiled=True
    )
    attention_deltas = lax.psum_scatter(
        jnp.concatenate([deltas.astype(low), delta_output.astype(low)], axis=1),
        "shard",
        scatter_dimension=0,
        tiled=True,
    )
    attention_deltas = lax.psum(attention_deltas, "rep").astype(full)
    gain_deltas = lax.psum(jnp.stack([delta_first, delta_second]), ("rep", "shard"))
    gain_deltas = lax.dynamic_slice_in_dim(
        gain_deltas, me * first_gain.shape[0], first_gain.shape[0], axis=1
    )
    return (
        out_tokens,
        delta_tokens,
        gain_deltas[0],
        attention_deltas[:, :query_width],
        attention_deltas[:, query_width : query_width + key_width],
        attention_deltas[:, query_width + key_width : inputs_width],
        attention_deltas[:, inputs_width:],
        gain_deltas[1],
        expert_deltas[0].astype(full),
        expert_deltas[1].astype(full),
        expert_deltas[2].astype(full),
    )


def solution(mesh):
    placed = (
        P(("rep", "shard"), None),
        P(("rep", "shard"), None),
        P(("rep", "shard"), None),
        P(("rep", "shard")),
        P(("rep", "shard")),
        P(("rep", "shard"), None),
        P(("rep", "shard"), None),
        P("shard"),
        P("shard", None),
        P("shard", None),
        P("shard", None),
        P("shard", None),
        P("shard"),
        P("shard", None, None),
        P("shard", None, None),
        P("shard", None, None),
    )
    return jax.shard_map(
        local,
        mesh=mesh,
        in_specs=placed,
        out_specs=(
            P(("rep", "shard"), None),
            P(("rep", "shard"), None),
            P("shard"),
            P("shard", None),
            P("shard", None),
            P("shard", None),
            P("shard", None),
            P("shard"),
            P("shard", None, None),
            P("shard", None, None),
            P("shard", None, None),
        ),
        check_vma=False,
    )
```

time: 1290 us -> 838 us (0.65); the launches traced: 1290 us -> 824 us
  waiting for transfers between devices: 711 us -> 396 us
  local copies, waits for them, and re-layouts: 185 us -> 63.4 us
  other arithmetic: 73.9 us -> 36.5 us
  starting transfers between devices: 39.4 us -> 9.02 us
  blocking collectives: 60 us -> 87.2 us
    all_to_all x7 -> x1, waiting for transfers between devices: 403 us -> 0.01 us  [local(): lax.all_to_all(input_slope[unpack_order], 'shard', split_axis=0, concat_a...]
    gather x8 -> x7, local copies, waits for them, and re-layouts: 122 us -> 19.6 us  [the longest x1 4.09 us: local(): normed_two_slope = back[pack_order].astype(full)]
    all_gather x4 -> x3, waiting for transfers between devices: 22 us -> 86.5 us  [the longest x1 44.8 us: local(): lax.all_gather(normed_two[unpack_order], 'shard', axis=0, tiled=True)]
    reduce_scatter x4 -> x3, waiting for transfers between devices: 94.5 us -> 147 us  [the longest x1 67 us: local(): lax.psum_scatter(swap(row_slopes.astype(low)), 'shard', scatter_dimension...]
    psum x1, blocking collectives: 14 us -> 57.3 us  [local(): lax.psum(jnp.stack([delta_first, delta_second]), ('rep', 'shard'))]
    scatter x2 -> x0, local copies, waits for them, and re-layouts: 31.2 us -> none  [the longest x1 15.7 us: local(): jnp.zeros((experts * capacity,), jnp.float32).at[target]]
    all_to_all x7 -> x1, starting transfers between devices: 33.8 us -> 3.56 us  [local(): lax.all_to_all(input_slope[unpack_order], 'shard', split_axis=0, concat_a...]
    psum x1, waiting for transfers between devices: 189 us -> 162 us  [local(): attention_deltas = lax.psum(attention_deltas, 'rep').astype(full)]
  transfers between devices with their start and end apart: 17 -> 9, of which waited for: 11 -> 7; matrix products, arithmetic and copies ran while one was open for 26% -> 16% of each run, Pallas kernels for 0% -> 0%
where the time goes in v1:
time: 838 us; the launch traced here: 824 us
  waiting for transfers between devices  396 us (47%)
  matrix products  216 us (26%)
  blocking collectives  87.2 us (10%)
  local copies, waits for them, and re-layouts  63.4 us (8%)
  other arithmetic  36.5 us (4%)
  between operations  15.3 us (2%)
  starting transfers between devices  9.02 us (1%)
    psum x1, waiting for transfers between devices, local(): attention_deltas = lax.psum(attention_deltas, 'rep').astype(full)  162 us
    reduce_scatter x1, waiting for transfers between devices, local(): lax.psum_scatter(swap(row_slopes.astype(low)), 'shard', scatter_dimension...  67 us
    reduce_scatter x1, waiting for transfers between devices, local(): lax.psum_scatter((result + shared.astype(full)).astype(low), 'shard', sca...  57.6 us
    psum x1, blocking collectives, local(): lax.psum(jnp.stack([delta_first, delta_second]), ('rep', 'shard'))  57.3 us
    all_gather x1, waiting for transfers between devices, local(): lax.all_gather(normed_two[unpack_order], 'shard', axis=0, tiled=True)  44.8 us
    dot_general x1, matrix products, local(): jnp.einsum('td,efd->etf', slope_rows, down_weight, preferred_element_type...  29.4 us
    all_gather x1, blocking collectives, local(): lax.all_gather(jnp.stack([first_gain, second_gain]), 'shard', axis=1, til...  22.5 us
    reduce_scatter x1, waiting for transfers between devices, local(): lax.psum_scatter(jnp.concatenate([deltas.astype(low), delta_output.astype...  22 us
  transfers between devices with their start and end apart: 9, of which 7 were waited for; matrix products, arithmetic and copies ran while one was open for 16% of the time, Pallas kernels for 0%

profile of v1, /device:TPU:0, one launch (start us, length us, event | category | flops | bytes accessed | tf_op | source)
XLA Modules:
  0.0 823.5 jit_solution(11777440212262105527)
XLA Ops:
  9.5 5.2 all-to-all-start.1
  15.2 22.5 %all_gather.15 = bf16[2,1024]{1,0:T(2,128)(2,1)S(1)} all-gather(bf16[2,128]{1,0:T(2,128)(2,1)S(1)} %pad_maximum_fusion.11), channel_id=1, replica_groups=mesh['rep'=4,'shard'=8] {'shard'}, dimensions={1}, use_global_device_ids=true | all-gather | bytes 4608 | tf_op jit(solution)/shard_map/all_gather | solution.py:186
  43.2 21.2 %all-gather.6.cloned.1.call-done = bf16[1024,3072]{1,0:T(8,128)(2,1)} async-done(((bf16[128,3072]{1,0:T(8,128)(2,1)}), bf16[1024,3072]{1,0:T(8,128)(2,1)}) %all-gather.6.cloned.1.call-update) | async-done | bytes 6291472 | tf_op jit(solution)/shard_map/all_gather | solution.py:176
  70.8 7.3 fusion.86
  78.2 8.2 fusion.15
  88.5 7.7 fusion.55
  106.4 7.4 all_to_all.33
  114.0 44.8 %all-gather.8.cloned.1.call-done = bf16[4096,1024]{1,0:T(8,128)(2,1)} async-done(((bf16[512,1024]{1,0:T(8,128)(2,1)}), bf16[4096,1024]{1,0:T(8,128)(2,1)}) %all-gather.8.cloned.1.call-update) | async-done | bytes 8388624 | tf_op jit(solution)/shard_map/all_gather | solution.py:231
  158.8 8.7 %copy.79 = bf16[8,8,64,1024]{3,2,0,1:T(8,128)(2,1)} copy(bf16[8,8,64,1024]{3,2,1,0:T(8,128)(2,1)} %bitcast.196) | data formatting | bytes 16777216 | tf_op jit(solution)/shard_map/reshape | solution.py:229
  167.5 15.4 %fusion.87 = f32[4096,2,512]{2,0,1:T(8,128)} fusion(bf16[4096,1024,1]{1,0,2:T(8,128)(2,1)} %bitcast.192, bf16[2,1024,512]{2,1,0:T(8,128)(2,1)S(1)} %copy-done.45), kind=kOutput, calls=%fused_computation.157 | convolution fusion | flops 8589934592 | bytes 27262976 | tf_op jit(solution)/shard_map/td,edf->etf/dot_general | solution.py:233
  182.8 11.7 %fusion.88 = f32[4096,2,512]{2,0,1:T(8,128)} fusion(bf16[4096,1024,1]{1,0,2:T(8,128)(2,1)S(1)} %bitcast.195, bf16[2,1024,512]{2,1,0:T(8,128)(2,1)S(1)} %copy-done.46), kind=kOutput, calls=%fused_computation.158 | convolution fusion | flops 8589934592 | bytes 27262976 | tf_op jit(solution)/shard_map/td,edf->etf/dot_general | solution.py:234
  194.5 20.6 %all-gather.10.cloned.1.call-done = bf16[4096,1024]{1,0:T(8,128)(2,1)} async-done(((bf16[512,1024]{1,0:T(8,128)(2,1)}), bf16[4096,1024]{1,0:T(8,128)(2,1)}) %all-gather.10.cloned.1.call-update) | async-done | bytes 8388624 | tf_op jit(solution)/shard_map/all_gather | solution.py:189
  215.1 29.4 %fusion.8 = (bf16[2,4096,512]{2,1,0:T(8,128)(2,1)}, bf16[2,4096,512]{2,1,0:T(8,128)(2,1)}, bf16[2,4096,512]{2,1,0:T(8,128)(2,1)}) fusion(f32[2,4096]{1,0:T(2,128)S(1)} %mul.348, f32[4096,2,512]{2,0,1:T(8,128)} %fusion.87, f32[4096,2,512]{2,0,1:T(8,128)} %fusion.88, bf16[2,512,1024]{2,1,0:T(8,128)(2,1)S(1)} %copy-done, ...), kind=kOutput, calls=%fused_computation.21 | convolution fusion | flops 8661237760 | bytes 69238784 | tf_op jit(solution)/shard_map/td,efd->etf/dot_general | solution.py:238
  244.5 16.7 %fusion.89 = f32[4096,1024,1]{1,0,2:T(8,128)} fusion(bf16[2,4096,512]{2,1,0:T(8,128)(2,1)} %get-tuple-element.106, bf16[2,1024,512]{2,1,0:T(8,128)(2,1)} %param.29), kind=kOutput, calls=%fused_computation.159 | convolution fusion | flops 8589934592 | bytes 27262976 | tf_op jit(solution)/shard_map/etf,edf->td/dot_general | solution.py:251
  261.2 17.1 %fusion.4 = bf16[4096,1024]{1,0:T(8,128)(2,1)} fusion(f32[4096,1024,1]{1,0,2:T(8,128)} %fusion.89, bf16[2,4096,512]{2,1,0:T(8,128)(2,1)} %get-tuple-element.105, bf16[2,1024,512]{2,1,0:T(8,128)(2,1)S(1)} %copy-done.47), kind=kOutput, calls=%fused_computation.15 | convolution fusion | flops 8598323200 | bytes 35651584 | tf_op jit(solution)/shard_map/etf,edf->td/dot_general | solution.py:252
  278.3 8.5 %copy.82 = bf16[8,8,64,1024]{3,2,1,0:T(8,128)(2,1)} copy(bf16[8,8,64,1024]{3,2,0,1:T(8,128)(2,1)} %bitcast.198) | data formatting | bytes 16777216 | tf_op jit(solution)/shard_map/transpose | solution.py:229
  291.2 67.0 %reduce-scatter.6.cloned.1.call-done = bf16[512,1024]{1,0:T(8,128)(2,1)} async-done(((bf16[4096,1024]{1,0:T(8,128)(2,1)}), bf16[512,1024]{1,0:T(8,128)(2,1)}) %reduce-scatter.6.cloned.1.call-update) | async-done | bytes 1048592 | tf_op jit(solution)/shard_map/reduce_scatter | solution.py:255
  373.3 15.7 %fusion.1 = (f32[8,2,512]{2,1,0:T(2,128)S(1)}, f32[8,512,512,2]{2,1,3,0:T(8,128)}) fusion(f32[8,2,512,512]{2,3,1,0:T(8,128)} %get-tuple-element.133, f32[8,2,512]{2,1,0:T(2,128)S(1)} %bitcast.219, bf16[512,8,64,1]{0,2,3,1:T(8,128)(2,1)} %bitcast.214, bf16[512,8,2,64]{0,3,2,1:T(8,128)(2,1)} %bitcast.190), kind=kOutput, calls=%fused_computation.11 | convolution fusion | flops 549445632 | bytes 35192832 | tf_op jit(solution)/shard_map/while/body/eval_jaxpr/igzd,jgd->gzij/dot_general | solution.py:105
  389.1 8.3 %fusion.3 = bf16[8,2,512,512]{2,3,1,0:T(8,128)(2,1)S(1)} fusion(f32[8,512,512,2]{2,1,3,0:T(8,128)} %get-tuple-element.137, f32[8,2,512,512]{2,3,1,0:T(8,128)S(1)} %bitcast.186, f32[8,2,512]{2,1,0:T(2,128)S(1)} %get-tuple-element.136, f32[8,2,512]{2,1,0:T(2,128)S(1)} %bitcast.220), kind=kLoop, calls=%fused_computation.13 | loop fusion | flops 16777216 | bytes 42008576 | tf_op jit(solution)/shard_map/while/body/eval_jaxpr/convert_element_type | solution.py:109
  403.6 7.0 fusion.63
  410.6 4.5 fusion.64
  426.2 14.8 %convert_bitcast_fusion = bf16[2,1024,512]{1,2,0:T(8,128)(2,1)} fusion(bf16[2,4096,512]{2,1,0:T(8,128)(2,1)} %get-tuple-element.105, bf16[4096,1024,1]{1,0,2:T(8,128)(2,1)} %bitcast.193), kind=kOutput, calls=%fused_computation.77 | convolution fusion | flops 8590983168 | bytes 18874368 | tf_op jit(solution)/shard_map/td,etf->edf/dot_general | solution.py:247
  441.0 14.9 %convert_bitcast_fusion.1 = bf16[2,1024,512]{1,2,0:T(8,128)(2,1)} fusion(bf16[2,4096,512]{2,1,0:T(8,128)(2,1)} %get-tuple-element.106, bf16[4096,1024,1]{1,0,2:T(8,128)(2,1)} %bitcast.194), kind=kOutput, calls=%fused_computation.78 | convolution fusion | flops 8590983168 | bytes 18874368 | tf_op jit(solution)/shard_map/td,etf->edf/dot_general | solution.py:246
  456.0 10.1 %fusion.46 = bf16[2,512,1024]{2,1,0:T(8,128)(2,1)} fusion(bf16[2,4096,512]{2,1,0:T(8,128)(2,1)S(1)} %bitcast.246, bf16[4096,1024]{1,0:T(8,128)(2,1)S(1)} %bitcast.227), kind=kOutput, calls=%fused_computation.82 | convolution fusion | flops 8590983168 | bytes 18874368 | tf_op jit(solution)/shard_map/etf,td->efd/dot_general | solution.py:245
  466.0 22.0 %reduce-scatter.8.cloned.1.call-done = bf16[128,3072]{1,0:T(8,128)(2,1)} async-done(((bf16[1024,3072]{1,0:T(8,128)(2,1)}), bf16[128,3072]{1,0:T(8,128)(2,1)}) %reduce-scatter.8.cloned.1.call-update) | async-done | bytes 786448 | tf_op jit(solution)/shard_map/reduce_scatter | solution.py:301
  492.4 14.8 %fusion = bf16[4096,1024]{1,0:T(8,128)(2,1)} fusion(bf16[4096,1024]{1,0:T(8,128)(2,1)S(1)} %bitcast.197, bf16[2,4096,512]{2,1,0:T(8,128)(2,1)} %get-tuple-element.107, bf16[2,512,1024]{2,1,0:T(8,128)(2,1)S(1)} %copy-done), kind=kOutput, calls=%fused_computation.8 | convolution fusion | flops 8602517504 | bytes 27262976 | tf_op jit(solution)/shard_map/etf,efd->td/dot_general | solution.py:259
  508.4 5.8 fusion.43
  521.2 57.3 %psum.35 = f32[2,1024]{1,0:T(2,128)S(1)} all-reduce(f32[2,1024]{1,0:T(2,128)S(1)} %pad_maximum_fusion.10), channel_id=1, replica_groups=mesh['rep'=4,'shard'=8] {'rep','shard'}, use_global_device_ids=true, to_apply=%region_15.16 | all-reduce | flops 2048 | bytes 16384 | tf_op jit(solution)/shard_map/psum | solution.py:308
  579.1 162.3 %all-reduce.3.cloned.1.call-done = (bf16[128,3072]{1,0:T(8,128)(2,1)}, bf16[2,1024,512]{1,2,0:T(8,128)(2,1)}, bf16[2,1024,512]{1,2,0:T(8,128)(2,1)}, bf16[2,512,1024]{2,1,0:T(8,128)(2,1)}) async-done(((bf16[128,3072]{1,0:T(8,128)(2,1)}, bf16[2,1024,512]{1,2,0:T(8,128)(2,1)}, bf16[2,1024,512]{1,2,0:T(8,128)(2,1)}, bf16[2,512,1024]{2,1,0:T(8,128)(2,1)}), (bf16[128,3072]{1,0:T(8,128)(2,1)}, ...) | async-done | bytes 7077904 | tf_op jit(solution)/shard_map/psum | solution.py:307
  745.5 4.1 copy.91
  749.6 4.3 copy.92
  758.0 57.6 %reduce-scatter.4.cloned.1.call-done = bf16[512,1024]{1,0:T(8,128)(2,1)} async-done(((bf16[4096,1024]{1,0:T(8,128)(2,1)}), bf16[512,1024]{1,0:T(8,128)(2,1)}) %reduce-scatter.4.cloned.1.call-update) | async-done | bytes 1048592 | tf_op jit(solution)/shard_map/reduce_scatter | solution.py:266
  (204 shorter events, 85.5 us)
Async XLA Ops:
  7.2 207.9 %copy-start = (bf16[2,512,1024]{2,1,0:T(8,128)(2,1)S(1)}, bf16[2,512,1024]{2,1,0:T(8,128)(2,1)}, u32[]{:S(2)}) copy-start(bf16[2,512,1024]{2,1,0:T(8,128)(2,1)} %param.31) | copy-start | bytes 6291460
  7.2 57.1 %all-gather.6.cloned.1.call-start = ((), (), s32[]{:S(2)}) async-start(), calls=%async_computation.6 | async-start | bytes 7077888 | tf_op jit(solution)/shard_map/all_gather | solution.py:176
  9.5 28.7 %all-to-all-start.1 = ((bf16[8,64,1024]{2,1,0:T(8,128)(2,1)}), bf16[8,64,1024]{2,1,0:T(8,128)(2,1)S(1)}, u32[]{:S(2)}, u32[]{:S(2)}) async-start(bf16[8,64,1024]{2,1,0:T(8,128)(2,1)} %bitcast.208), calls=%async_computation.1 | async-start | bytes 2097152 | tf_op jit(solution)/shard_map/all_to_all | solution.py:171
  14.7 144.1 %all-gather.8.cloned.1.call-start = ((), (), s32[]{:S(2)}) async-start(), calls=%async_computation.10 | async-start | bytes 9437184 | tf_op jit(solution)/shard_map/all_gather | solution.py:231
  15.0 26.1 %copy-start.34 = (s32[1024]{0:T(1024)}, s32[1024]{0:T(1024)S(1)}, u32[]{:S(2)}) copy-start(s32[1024]{0:T(1024)S(1)} %pad_clamp_fusion) | copy-start | bytes 12292
  15.0 90.2 %copy-start.32 = (s32[1024]{0:T(1024)}, s32[1024]{0:T(1024)S(1)}, u32[]{:S(2)}) copy-start(s32[1024]{0:T(1024)S(1)} %pad_clamp_fusion.1) | copy-start | bytes 12292
  37.7 48.7 %copy-start.38 = (f32[1,1024]{1,0:T(1,128)}, f32[1,1024]{1,0:T(1,128)S(1)}, u32[]{:S(2)}) copy-start(f32[1,1024]{1,0:T(1,128)S(1)} %get-tuple-element.123) | copy-start | bytes 12292
  38.1 32.6 %copy-start.19 = (f32[512,32]{0,1:T(8,128)}, f32[512,32]{0,1:T(8,128)S(1)}, u32[]{:S(2)}) copy-start(f32[512,32]{0,1:T(8,128)S(1)} %get-tuple-element.124) | copy-start | bytes 196612
  38.1 32.6 %copy-start.21 = (f32[512,32]{0,1:T(8,128)}, f32[512,32]{0,1:T(8,128)S(1)}, u32[]{:S(2)}) copy-start(f32[512,32]{0,1:T(8,128)S(1)} %get-tuple-element.125) | copy-start | bytes 196612
  43.2 43.2 %copy-start.41 = (f32[512]{0:T(512)}, f32[512]{0:T(512)S(1)}, u32[]{:S(2)}) copy-start(f32[512]{0:T(512)S(1)} %get-tuple-element.127) | copy-start | bytes 6148
  104.2 110.9 %all-gather.10.cloned.1.call-start = ((), (), s32[]{:S(2)}) async-start(), calls=%async_computation.11 | async-start | bytes 9437184 | tf_op jit(solution)/shard_map/all_gather | solution.py:189
  105.0 253.3 %reduce-scatter.6.cloned.1.call-start = ((), (), s32[]{:S(2)}) async-start(), calls=%async_computation.8 | async-start | bytes 9437184 | tf_op jit(solution)/shard_map/reduce_scatter | solution.py:255
  167.5 15.4 %copy-start.11 = (bf16[8,8,64,1024]{3,2,0,1:T(8,128)(2,1)S(1)}, bf16[8,8,64,1024]{3,2,0,1:T(8,128)(2,1)}, u32[]{:S(2)}) copy-start(bf16[8,8,64,1024]{3,2,0,1:T(8,128)(2,1)} %copy.79) | copy-start | bytes 25165828
  167.5 15.4 %copy-start.46 = (bf16[2,1024,512]{2,1,0:T(8,128)(2,1)S(1)}, bf16[2,1024,512]{2,1,0:T(8,128)(2,1)}, u32[]{:S(2)}) copy-start(bf16[2,1024,512]{2,1,0:T(8,128)(2,1)} %param.30) | copy-start | bytes 6291460
  244.5 16.7 %copy-start.47 = (bf16[2,1024,512]{2,1,0:T(8,128)(2,1)S(1)}, bf16[2,1024,512]{2,1,0:T(8,128)(2,1)}, u32[]{:S(2)}) copy-start(bf16[2,1024,512]{2,1,0:T(8,128)(2,1)} %param.30) | copy-start | bytes 6291460
  286.8 201.2 %reduce-scatter.8.cloned.1.call-start = ((), (), s32[]{:S(2)}) async-start(), calls=%async_computation.9 | async-start | bytes 7077888 | tf_op jit(solution)/shard_map/reduce_scatter | solution.py:301
  286.9 102.2 %copy-start.31 = (f32[2,8,512]{2,1,0:T(8,128)}, f32[2,8,512]{2,1,0:T(8,128)S(1)}, u32[]{:S(2)}) copy-start(f32[2,8,512]{2,1,0:T(8,128)S(1)} %log_add_fusion) | copy-start | bytes 98308
  373.3 15.7 %slice-start = ((s8[16777216]{0:T(1024)(128)(4,1)}), s8[4194304]{0:T(1024)(128)(4,1)S(1)}, s32[]{:S(2)}) async-start(s8[16777216]{0:T(1024)(128)(4,1)} %bitcast.185), calls=%async_computation.13 | async-start | bytes 8388608
  373.3 15.7 %slice-start.1 = ((s8[16777216]{0:T(1024)(128)(4,1)}), s8[4194304]{0:T(1024)(128)(4,1)S(1)}, s32[]{:S(2)}) async-start(s8[16777216]{0:T(1024)(128)(4,1)} %bitcast.185), calls=%async_computation.14 | async-start | bytes 8388608
  373.3 15.8 %slice-start.2 = ((s8[16777216]{0:T(1024)(128)(4,1)}), s8[4194304]{0:T(1024)(128)(4,1)S(1)}, s32[]{:S(2)}) async-start(s8[16777216]{0:T(1024)(128)(4,1)} %bitcast.185), calls=%async_computation.15 | async-start | bytes 8388608
  373.3 15.8 %slice-start.3 = ((s8[16777216]{0:T(1024)(128)(4,1)}), s8[4194304]{0:T(1024)(128)(4,1)S(1)}, s32[]{:S(2)}) async-start(s8[16777216]{0:T(1024)(128)(4,1)} %bitcast.185), calls=%async_computation.16 | async-start | bytes 8388608
  389.1 11.7 %copy-start.25 = (bf16[512,8,32]{0,2,1:T(8,128)(2,1)S(1)}, bf16[512,8,32]{0,2,1:T(8,128)(2,1)}, u32[]{:S(2)}) copy-start(bf16[512,8,32]{0,2,1:T(8,128)(2,1)} %copy-done.24) | copy-start | bytes 786436
  389.1 11.7 %copy-start.27 = (bf16[512,8,32]{0,2,1:T(8,128)(2,1)S(1)}, bf16[512,8,32]{0,2,1:T(8,128)(2,1)}, u32[]{:S(2)}) copy-start(bf16[512,8,32]{0,2,1:T(8,128)(2,1)} %copy-done.26) | copy-start | bytes 786436
  426.1 315.3 %all-reduce.3.cloned.1.call-start = ((), (), s32[]{:S(2)}) async-start(), calls=%async_computation.12 | async-start | bytes 14155776 | tf_op jit(solution)/shard_map/psum | solution.py:307
  426.2 29.8 %slice-start.4 = ((s8[8388608]{0:T(1024)(128)(4,1)}), s8[4194304]{0:T(1024)(128)(4,1)S(1)}, s32[]{:S(2)}) async-start(s8[8388608]{0:T(1024)(128)(4,1)} %bitcast.226), calls=%async_computation.17 | async-start | bytes 8388608
  426.2 29.8 %slice-start.6 = ((s8[8388608]{0:T(1024)(128)(4,1)}), s8[4194304]{0:T(1024)(128)(4,1)S(1)}, s32[]{:S(2)}) async-start(s8[8388608]{0:T(1024)(128)(4,1)} %bitcast.245), calls=%async_computation.19 | async-start | bytes 8388608
  441.0 14.9 %slice-start.5 = ((s8[8388608]{0:T(1024)(128)(4,1)}), s8[4194304]{0:T(1024)(128)(4,1)S(1)}, s32[]{:S(2)}) async-start(s8[8388608]{0:T(1024)(128)(4,1)} %bitcast.226), calls=%async_computation.18 | async-start | bytes 8388608
  441.0 14.9 %slice-start.7 = ((s8[8388608]{0:T(1024)(128)(4,1)}), s8[4194304]{0:T(1024)(128)(4,1)S(1)}, s32[]{:S(2)}) async-start(s8[8388608]{0:T(1024)(128)(4,1)} %bitcast.245), calls=%async_computation.20 | async-start | bytes 8388608
  466.0 22.0 %copy-start.2 = (bf16[512,1024]{1,0:T(8,128)(2,1)S(1)}, bf16[512,1024]{1,0:T(8,128)(2,1)}, u32[]{:S(2)}) copy-start(bf16[512,1024]{1,0:T(8,128)(2,1)} %get-tuple-element.113) | copy-start | bytes 3145732
  466.0 22.0 %copy-start.33 = (s32[1024]{0:T(1024)S(1)}, s32[1024]{0:T(1024)}, u32[]{:S(2)}) copy-start(s32[1024]{0:T(1024)} %copy-done.32) | copy-start | bytes 12292
  488.0 327.5 %reduce-scatter.4.cloned.1.call-start = ((), (), s32[]{:S(2)}) async-start(), calls=%async_computation.7 | async-start | bytes 9437184 | tf_op jit(solution)/shard_map/reduce_scatter | solution.py:266
  517.6 61.4 %all-to-all-start.2 = ((bf16[8,64,1024]{2,1,0:T(8,128)(2,1)}), bf16[8,64,1024]{2,1,0:T(8,128)(2,1)S(1)}, u32[]{:S(2)}, u32[]{:S(2)}) async-start(bf16[8,64,1024]{2,1,0:T(8,128)(2,1)} %bitcast.201), calls=%async_computation.4 | async-start | bytes 2097152 | tf_op jit(solution)/shard_map/all_to_all | solution.py:298
  (37 other events, 168.4 us)
Sparse Core Ops, SparseCore 0:
  10.5 53.7 all-gather.5
  104.4 54.3 all-gather.7
  160.7 54.3 all-gather.9
  286.9 71.2 reduce-scatter.5
  426.2 61.7 reduce-scatter.7
  491.0 250.2 all-reduce.2
  745.4 70.0 reduce-scatter.3

commit v2 on v1

--- a/solution.py
+++ b/solution.py
@@ -1,6 +1,10 @@
+import functools
+
 import jax
 import jax.numpy as jnp
 from jax import lax
+from jax.experimental import pallas as pl
+from jax.experimental.pallas import tpu as pltpu
 from jax.sharding import PartitionSpec as P
 
 QUERY_HEADS = 16
@@ -142,6 +146,729 @@
         inputs * scaled, axis=1, keepdims=True
     )
     return (input_slope, gain_slope)
+
+MESH = pl.DeviceIdType.MESH
+NN = (((1,), (0,)), ((), ()))
+NT = (((1,), (1,)), ((), ()))
+TN = (((0,), (0,)), ((), ()))
+TILE = 256
+VMEM_MOST = 66_000_000
+
+
+def matmul(left, right, dims):
+    return lax.dot_general(left, right, dims, preferred_element_type=jnp.float32)
+
+
+def flip(number, mask, count):
+    out = 0
+    bit = 1
+    while bit < count:
+        a = (number // bit) % 2
+        b = (mask // bit) % 2
+        out = out + (a + b - 2 * a * b) * bit
+        bit *= 2
+    return out
+
+
+def greet(me, rep, count):
+    barrier = pltpu.get_barrier_semaphore()
+    for k in range(1, count):
+        pl.semaphore_signal(
+            barrier, inc=1, device_id=(rep, lax.rem(me + k, count)), device_id_type=MESH
+        )
+    pl.semaphore_wait(barrier, count - 1)
+
+
+def expert_kernel(
+    count,
+    own_ref,
+    slope_ref,
+    mix_ref,
+    gate_ref,
+    up_ref,
+    down_ref,
+    hidden_out,
+    grad_out,
+    delta_gate_ref,
+    delta_up_ref,
+    delta_down_ref,
+    rows,
+    slope_buf,
+    hidden_buf,
+    grad_buf,
+    acc_gate,
+    acc_up,
+    acc_down,
+    send_sem,
+    recv_sem,
+    own_sem,
+    slope_sem,
+    hidden_sem,
+    grad_sem,
+):
+    rep = lax.axis_index("rep")
+    me = lax.axis_index("shard")
+    experts, width, hidden = gate_ref.shape
+    tokens = own_ref.shape[0]
+    low = jnp.bfloat16
+
+    def remote(source, slot, index, target):
+        return pltpu.make_async_remote_copy(
+            src_ref=source,
+            dst_ref=rows.at[slot],
+            send_sem=send_sem.at[index],
+            recv_sem=recv_sem.at[index],
+            device_id=(rep, target),
+            device_id_type=MESH,
+        )
+
+    def slope_copy(k):
+        return pltpu.make_async_copy(
+            slope_ref.at[:, flip(me, k, count)], slope_buf.at[k % 2], slope_sem.at[k % 2]
+        )
+
+    def hidden_copy(k):
+        return pltpu.make_async_copy(
+            hidden_buf.at[k % 2], hidden_out.at[flip(me, k, count)], hidden_sem.at[k % 2]
+        )
+
+    def grad_copy(k):
+        return pltpu.make_async_copy(
+            grad_buf.at[k % 2], grad_out.at[flip(me, k, count)], grad_sem.at[k % 2]
+        )
+
+    slope_copy(0).start()
+    own = pltpu.make_async_copy(own_ref, rows.at[me], own_sem)
+    own.start()
+    greet(me, rep, count)
+    for k in [1] + list(range(2, count, 2)):
+        remote(own_ref, me, k, flip(me, k, count)).start()
+    own.wait()
+
+    def step(k, carry):
+        pack = flip(me, k, count)
+
+        @pl.when(k >= 1)
+        def _():
+            remote(own_ref, pack, k, me).wait_recv()
+
+        @pl.when((k >= 2) & (k % 2 == 0))
+        def _():
+            remote(rows.at[pack], pack, k + 1, flip(me, 1, count)).start()
+
+        @pl.when(k + 1 < count)
+        def _():
+            slope_copy(k + 1).start()
+
+        slope_copy(k).wait()
+
+        @pl.when(k >= 2)
+        def _():
+            hidden_copy(k - 2).wait()
+            grad_copy(k - 2).wait()
+
+        slot = k % 2
+        x = rows[pack]
+        dy = slope_buf[slot].reshape(tokens, width)
+        for e in range(experts):
+            mix = mix_ref[pack, :, e : e + 1]
+            for part in range(hidden // TILE):
+                span = pl.ds(part * TILE, TILE)
+                ga = matmul(x, gate_ref[e, :, span], NN)
+                ua = matmul(x, up_ref[e, :, span], NN)
+                dh = matmul(dy, down_ref[e, span, :], NT) * mix
+                sig = jax.nn.sigmoid(ga)
+                act = ga * sig
+                out = pl.ds(e * hidden + part * TILE, TILE)
+                hidden_buf[slot, :, out] = (mix * (act * ua)).astype(low)
+                grad_buf[slot, :, out] = (dh * ua * sig * (1.0 + ga * (1.0 - sig))).astype(low)
+                grad_buf[
+                    slot, :, pl.ds(experts * hidden + e * hidden + part * TILE, TILE)
+                ] = (dh * act).astype(low)
+        hidden_copy(k).start()
+        grad_copy(k).start()
+
+        def add(acc, value):
+            @pl.when(k == 0)
+            def _():
+                acc[...] = value
+
+            @pl.when(k > 0)
+            def _():
+                acc[...] += value
+
+        half = experts * hidden
+        add(acc_gate, matmul(x, grad_buf[slot, :, :half], TN))
+        add(acc_up, matmul(x, grad_buf[slot, :, half:], TN))
+        add(acc_down, matmul(hidden_buf[slot], dy, TN))
+        return carry
+
+    lax.fori_loop(0, count, step, 0)
+    for e in range(experts):
+        span = pl.ds(e * hidden, hidden)
+        delta_gate_ref[e] = acc_gate[:, span].astype(low)
+        delta_up_ref[e] = acc_up[:, span].astype(low)
+        delta_down_ref[e] = acc_down[span, :].astype(low)
+    for k in (count - 2, count - 1):
+        hidden_copy(k).wait()
+        grad_copy(k).wait()
+    for k in range(1, count):
+        remote(own_ref, me, k, me).wait_send()
+
+
+def expert_pass(normed, all_slopes, mixing, gate_weight, up_weight, down_weight, count):
+    tokens, width = normed.shape
+    experts, _, hidden = gate_weight.shape
+    block = tokens // count
+    low = jnp.bfloat16
+    anywhere = pl.BlockSpec(memory_space=pl.ANY)
+    inside = pl.BlockSpec(memory_space=pltpu.VMEM)
+    flops = 2 * count * tokens * width * hidden * experts * 6
+    return pl.pallas_call(
+        functools.partial(expert_kernel, count),
+        name="expert_pass",
+        out_shape=(
+            jax.ShapeDtypeStruct((count, tokens, experts * hidden), low),
+            jax.ShapeDtypeStruct((count, tokens, 2 * experts * hidden), low),
+            jax.ShapeDtypeStruct(gate_weight.shape, low),
+            jax.ShapeDtypeStruct(up_weight.shape, low),
+            jax.ShapeDtypeStruct(down_weight.shape, low),
+        ),
+        in_specs=[inside, anywhere, inside, inside, inside, inside],
+        out_specs=(anywhere, anywhere, inside, inside, inside),
+        scratch_shapes=[
+            pltpu.VMEM((count, tokens, width), low),
+            pltpu.VMEM((2, count, block, width), low),
+            pltpu.VMEM((2, tokens, experts * hidden), low),
+            pltpu.VMEM((2, tokens, 2 * experts * hidden), low),
+            pltpu.VMEM((width, experts * hidden), jnp.float32),
+            pltpu.VMEM((width, experts * hidden), jnp.float32),
+            pltpu.VMEM((experts * hidden, width), jnp.float32),
+            pltpu.SemaphoreType.DMA((count,)),
+            pltpu.SemaphoreType.DMA((count,)),
+            pltpu.SemaphoreType.DMA,
+            pltpu.SemaphoreType.DMA((2,)),
+            pltpu.SemaphoreType.DMA((2,)),
+            pltpu.SemaphoreType.DMA((2,)),
+        ],
+        compiler_params=pltpu.CompilerParams(
+            collective_id=1, has_side_effects=True, vmem_limit_bytes=VMEM_MOST
+        ),
+        cost_estimate=pl.CostEstimate(flops=flops, bytes_accessed=1 << 26, transcendentals=0),
+    )(
+        normed,
+        all_slopes.reshape(count, count, block, width),
+        mixing,
+        gate_weight,
+        up_weight,
+        down_weight,
+    )
+
+
+def return_kernel(
+    count,
+    grad_ref,
+    hidden_ref,
+    gate_ref,
+    up_ref,
+    down_ref,
+    own_ref,
+    back_ref,
+    out_ref,
+    grad_buf,
+    hidden_buf,
+    pair_send,
+    far_send,
+    pair_recv,
+    far_recv,
+    total,
+    load_sem,
+    pair_send_sem,
+    pair_recv_sem,
+    far_send_sem,
+    far_recv_sem,
+):
+    rep = lax.axis_index("rep")
+    me = lax.axis_index("shard")
+    experts, width, hidden = gate_ref.shape
+    tokens = own_ref.shape[0]
+    block = tokens // count
+    low = jnp.bfloat16
+    pairs = count // 2
+    partner = flip(me, 1, count)
+    greet(me, rep, count)
+
+    def reduce(phase, load, part, base):
+        def pair_copy(turn):
+            return pltpu.make_async_remote_copy(
+                src_ref=pair_send.at[turn % 2],
+                dst_ref=pair_recv.at[base + turn],
+                send_sem=pair_send_sem.at[turn % 2],
+                recv_sem=pair_recv_sem.at[base + turn],
+                device_id=(rep, partner),
+                device_id_type=MESH,
+            )
+
+        def far_copy(turn, target):
+            return pltpu.make_async_remote_copy(
+                src_ref=far_send.at[turn % 2],
+                dst_ref=far_recv.at[base + turn],
+                send_sem=far_send_sem.at[turn % 2],
+                recv_sem=far_recv_sem.at[base + turn],
+                device_id=(rep, target),
+                device_id_type=MESH,
+            )
+
+        load(0).start()
+
+        def turn_step(turn, carry):
+            mask = count - 2 - 2 * turn
+            load(2 * turn + 1).start()
+            load(2 * turn).wait()
+            value = part(0, flip(me, mask + 1, count))
+
+            @pl.when(turn >= 2)
+            def _():
+                pair_copy(turn - 2).wait_send()
+
+            pair_send[turn % 2] = value.astype(low)
+            pair_copy(turn).start()
+
+            @pl.when(turn + 1 < pairs)
+            def _():
+                load(2 * turn + 2).start()
+
+            load(2 * turn + 1).wait()
+            total[...] = part(1, flip(me, mask, count))
+            pair_copy(turn).wait_recv()
+
+            @pl.when(turn + 1 < pairs)
+            def _():
+                @pl.when(turn >= 2)
+                def _():
+                    far_copy(turn - 2, me).wait_send()
+
+                far_send[turn % 2] = (
+                    total[...] + pair_recv[base + turn].astype(jnp.float32)
+                ).astype(low)
+                far_copy(turn, flip(me, mask, count)).start()
+
+            return carry
+
+        lax.fori_loop(0, pairs, turn_step, 0)
+        total[...] += pair_recv[base + pairs - 1].astype(jnp.float32)
+
+        def finish():
+            def add(turn, carry):
+                far_copy(turn, me).wait_recv()
+                total[...] += far_recv[base + turn].astype(jnp.float32)
+                return carry
+
+            lax.fori_loop(0, pairs - 1, add, 0)
+            for turn in range(max(0, pairs - 2), pairs):
+                pair_copy(turn).wait_send()
+            for turn in range(max(0, pairs - 3), pairs - 1):
+                far_copy(turn, me).wait_send()
+
+        finish()
+
+    def target(item):
+        turn = item // 2
+        mask = count - 2 - 2 * turn + 1 - item % 2
+        return flip(me, mask, count)
+
+    def grad_load(item):
+        return pltpu.make_async_copy(
+            grad_ref.at[target(item)], grad_buf.at[item % 2], load_sem.at[item % 2]
+        )
+
+    def grad_part(slot, pack):
+        value = None
+        for e in range(experts):
+            for at, weight in ((e, gate_ref), (experts + e, up_ref)):
+                term = matmul(grad_buf[slot, :, pl.ds(at * hidden, hidden)], weight[e], NT)
+                value = term if value is None else value + term
+        return value
+
+    def hidden_load(item):
+        return pltpu.make_async_copy(
+            hidden_ref.at[:, target(item)], hidden_buf.at[item % 2], load_sem.at[item % 2]
+        )
+
+    def hidden_part(slot, pack):
+        value = None
+        for e in range(experts):
+            term = matmul(
+                hidden_buf[slot, :, :, pl.ds(e * hidden, hidden)].reshape(tokens, hidden),
+                down_ref[e],
+                NN,
+            )
+            value = term if value is None else value + term
+        total[...] = value
+        mine = pl.ds(pl.multiple_of(me * block, block), block)
+        theirs = pl.ds(pl.multiple_of(pack * block, block), block)
+        total[mine, :] += own_ref[theirs, :]
+        return total[...]
+
+    reduce(0, grad_load, grad_part, 0)
+    back_ref[...] = total[...]
+    reduce(1, hidden_load, hidden_part, pairs)
+    out_ref[...] = total[...].astype(low)
+
+
+def return_pass(grads, hiddens, gate_weight, up_weight, down_weight, own, count):
+    tokens, width = own.shape
+    experts, _, hidden = gate_weight.shape
+    block = tokens // count
+    low = jnp.bfloat16
+    pairs = count // 2
+    anywhere = pl.BlockSpec(memory_space=pl.ANY)
+    inside = pl.BlockSpec(memory_space=pltpu.VMEM)
+    flops = 2 * count * tokens * width * hidden * experts * 3
+    return pl.pallas_call(
+        functools.partial(return_kernel, count),
+        name="return_pass",
+        out_shape=(
+            jax.ShapeDtypeStruct((tokens, width), jnp.float32),
+            jax.ShapeDtypeStruct((tokens, width), low),
+        ),
+        in_specs=[anywhere, anywhere, inside, inside, inside, inside],
+        out_specs=(inside, inside),
+        scratch_shapes=[
+            pltpu.VMEM((2, tokens, 2 * experts * hidden), low),
+            pltpu.VMEM((2, count, block, experts * hidden), low),
+            pltpu.VMEM((2, tokens, width), low),
+            pltpu.VMEM((2, tokens, width), low),
+            pltpu.VMEM((2 * pairs, tokens, width), low),
+            pltpu.VMEM((2 * pairs, tokens, width), low),
+            pltpu.VMEM((tokens, width), jnp.float32),
+            pltpu.SemaphoreType.DMA((2,)),
+            pltpu.SemaphoreType.DMA((2,)),
+            pltpu.SemaphoreType.DMA((2 * pairs,)),
+            pltpu.SemaphoreType.DMA((2,)),
+            pltpu.SemaphoreType.DMA((2 * pairs,)),
+        ],
+        compiler_params=pltpu.CompilerParams(
+            collective_id=2, has_side_effects=True, vmem_limit_bytes=VMEM_MOST
+        ),
+        cost_estimate=pl.CostEstimate(flops=flops, bytes_accessed=1 << 26, transcendentals=0),
+    )(
+        grads,
+        hiddens.reshape(count, count, block, experts * hidden),
+        gate_weight,
+        up_weight,
+        down_weight,
+        own,
+    )
+
+
+def settle_kernel(
+    count,
+    reps,
+    delta_ref,
+    gain_ref,
+    slope_ref,
+    delta_out,
+    gain_out,
+    slope_out,
+    pair_recv,
+    far_send,
+    far_recv,
+    piece,
+    line_recv,
+    line_send,
+    gain_recv,
+    gain_sum,
+    gain_line,
+    pair_send_sem,
+    pair_recv_sem,
+    far_send_sem,
+    far_recv_sem,
+    line_send_sem,
+    line_recv_sem,
+    gain_send_sem,
+    gain_recv_sem,
+    gain_line_send,
+    gain_line_recv,
+    slope_send_sem,
+    slope_recv_sem,
+    own_sem,
+):
+    rep = lax.axis_index("rep")
+    me = lax.axis_index("shard")
+    low = jnp.bfloat16
+    full = jnp.float32
+    rows = piece.shape[0]
+    pairs = count // 2
+    partner = flip(me, 1, count)
+    barrier = pltpu.get_barrier_semaphore()
+    for k in range(1, count):
+        pl.semaphore_signal(
+            barrier, inc=1, device_id=(rep, lax.rem(me + k, count)), device_id_type=MESH
+        )
+    for k in range(1, reps):
+        pl.semaphore_signal(
+            barrier, inc=1, device_id=(lax.rem(rep + k, reps), me), device_id_type=MESH
+        )
+    pl.semaphore_wait(barrier, count + reps - 2)
+
+    def copy(source, target, sends, recvs, device):
+        return pltpu.make_async_remote_copy(
+            src_ref=source,
+            dst_ref=target,
+            send_sem=sends,
+            recv_sem=recvs,
+            device_id=device,
+            device_id_type=MESH,
+        )
+
+    def block(owner):
+        return pl.ds(pl.multiple_of(owner * rows, rows), rows)
+
+    def pair_copy(turn):
+        owner = flip(partner, 2 * turn, count)
+        return copy(
+            delta_ref.at[block(owner)],
+            pair_recv.at[turn],
+            pair_send_sem.at[turn],
+            pair_recv_sem.at[turn],
+            (rep, partner),
+        )
+
+    def far_copy(turn):
+        return copy(
+            far_send.at[turn],
+            far_recv.at[turn],
+            far_send_sem.at[turn],
+            far_recv_sem.at[turn],
+            (rep, flip(me, 2 * turn, count)),
+        )
+
+    def gain_copy(k):
+        target = flip(me, k, count)
+        return copy(
+            gain_ref.at[target],
+            gain_recv.at[k],
+            gain_send_sem.at[k],
+            gain_recv_sem.at[k],
+            (rep, target),
+        )
+
+    def slope_copy(k):
+        target = flip(me, k, count)
+        return copy(
+            slope_ref.at[target],
+            slope_out.at[me],
+            slope_send_sem.at[k],
+            slope_recv_sem.at[k],
+            (rep, target),
+        )
+
+    def gain_line_copy(k):
+        return copy(
+            gain_sum,
+            gain_line.at[rep],
+            gain_line_send.at[k],
+            gain_line_recv.at[k],
+            (lax.rem(rep + k, reps), me),
+        )
+
+    order = list(range(pairs - 1, 0, -1)) + [0]
+    for turn in order:
+        pair_copy(turn).start()
+    for k in range(1, count):
+        gain_copy(k).start()
+    own = pltpu.make_async_copy(slope_ref.at[me], slope_out.at[me], own_sem)
+    own.start()
+    for turn in order[:-1]:
+        pair_copy(turn).wait_recv()
+        mine = delta_ref[block(flip(me, 2 * turn, count)), :].astype(full)
+        far_send[turn] = (mine + pair_recv[turn].astype(full)).astype(low)
+        far_copy(turn).start()
+    for k in range(count - 1, 0, -1):
+        slope_copy(k).start()
+    total = gain_ref[me]
+    for k in range(1, count):
+        gain_copy(k).wait_recv()
+        total = total + gain_recv[k]
+    gain_sum[...] = total
+    gain_line[rep] = total
+    for k in range(1, reps):
+        gain_line_copy(k).start()
+    pair_copy(0).wait_recv()
+    for turn in range(1, pairs):
+        far_copy(turn).wait_recv()
+
+    segments = 4
+    size = rows // segments
+
+    def span(i):
+        return pl.ds(i * size, size)
+
+    for i in range(segments):
+        value = delta_ref[
+            pl.ds(pl.multiple_of(me * rows + i * size, size), size), :
+        ].astype(full)
+        for turn in range(pairs):
+            source = pair_recv if turn == 0 else far_recv
+            value = value + source[turn, span(i), :].astype(full)
+        piece[span(i), :] = value.astype(low)
+
+    if reps == 4:
+        outer = (rep == 0) | (rep == reps - 1)
+        inside = jnp.where(rep == 0, 1, 2)
+        outside = jnp.where(rep == 1, 0, 3)
+        across = 3 - rep
+
+        def up_copy(i):
+            return copy(
+                piece.at[span(i)],
+                line_recv.at[0, span(i)],
+                line_send_sem.at[0, i],
+                line_recv_sem.at[0, i],
+                (inside, me),
+            )
+
+        def across_copy(i):
+            return copy(
+                line_send.at[0, span(i)],
+                line_recv.at[1, span(i)],
+                line_send_sem.at[1, i],
+                line_recv_sem.at[1, i],
+                (across, me),
+            )
+
+        def down_copy(i):
+            return copy(
+                line_send.at[1, span(i)],
+                line_recv.at[2, span(i)],
+                line_send_sem.at[2, i],
+                line_recv_sem.at[2, i],
+                (outside, me),
+            )
+
+        @pl.when(outer)
+        def _():
+            for i in range(segments):
+                up_copy(i).start()
+            for i in range(segments):
+                down_copy(i).wait_recv()
+                delta_out[span(i), :] = line_recv[2, span(i), :].astype(full)
+            for i in range(segments):
+                up_copy(i).wait_send()
+
+        @pl.when(jnp.logical_not(outer))
+        def _():
+            for i in range(segments + 1):
+                if i < segments:
+                    up_copy(i).wait_recv()
+                    both = piece[span(i), :].astype(full) + line_recv[0, span(i), :].astype(full)
+                    line_send[0, span(i), :] = both.astype(low)
+                    across_copy(i).start()
+                if i > 0:
+                    j = i - 1
+                    across_copy(j).wait_recv()
+                    every = line_send[0, span(j), :].astype(full) + line_recv[
+                        1, span(j), :
+                    ].astype(full)
+                    line_send[1, span(j), :] = every.astype(low)
+                    down_copy(j).start()
+                    delta_out[span(j), :] = every.astype(low).astype(full)
+            for i in range(segments):
+                across_copy(i).wait_send()
+                down_copy(i).wait_send()
+    else:
+
+        def spread_copy(k):
+            return copy(
+                piece,
+                line_recv.at[rep],
+                line_send_sem.at[k],
+                line_recv_sem.at[k],
+                (lax.rem(rep + k, reps), me),
+            )
+
+        for k in range(1, reps):
+            spread_copy(k).start()
+        line_recv[rep] = piece[...]
+        for k in range(1, reps):
+            spread_copy(k).wait_recv()
+        value = line_recv[0].astype(full)
+        for k in range(1, reps):
+            value = value + line_recv[k].astype(full)
+        delta_out[...] = value
+        for k in range(1, reps):
+            spread_copy(k).wait_send()
+
+    for k in range(1, reps):
+        gain_line_copy(k).wait_recv()
+    total = gain_line[0]
+    for k in range(1, reps):
+        total = total + gain_line[k]
+    gain_out[...] = total
+    own.wait()
+    for k in range(1, count):
+        slope_copy(k).wait_recv()
+    for k in range(1, count):
+        slope_copy(k).wait_send()
+        gain_copy(k).wait_send()
+    for turn in range(pairs):
+        pair_copy(turn).wait_send()
+    for turn in range(1, pairs):
+        far_copy(turn).wait_send()
+    for k in range(1, reps):
+        gain_line_copy(k).wait_send()
+
+
+def settle_pass(deltas, gains, slopes, count, reps):
+    width, columns = deltas.shape
+    rows = width // count
+    tokens = slopes.shape[0]
+    pairs = count // 2
+    low = jnp.bfloat16
+    full = jnp.float32
+    dma = pltpu.SemaphoreType.DMA
+    inside = pl.BlockSpec(memory_space=pltpu.VMEM)
+    line = (3, 4) if reps == 4 else (reps,)
+    return pl.pallas_call(
+        functools.partial(settle_kernel, count, reps),
+        name="settle_pass",
+        out_shape=(
+            jax.ShapeDtypeStruct((rows, columns), full),
+            jax.ShapeDtypeStruct((8, rows), full),
+            jax.ShapeDtypeStruct((count, tokens // count, width), low),
+        ),
+        in_specs=[inside, inside, inside],
+        out_specs=(inside, inside, inside),
+        scratch_shapes=[
+            pltpu.VMEM((pairs, rows, columns), low),
+            pltpu.VMEM((pairs, rows, columns), low),
+            pltpu.VMEM((pairs, rows, columns), low),
+            pltpu.VMEM((rows, columns), low),
+            pltpu.VMEM((3 if reps == 4 else reps, rows, columns), low),
+            pltpu.VMEM((2, rows, columns), low),
+            pltpu.VMEM((count, 8, rows), full),
+            pltpu.VMEM((8, rows), full),
+            pltpu.VMEM((reps, 8, rows), full),
+            dma((pairs,)),
+            dma((pairs,)),
+            dma((pairs,)),
+            dma((pairs,)),
+            dma(line),
+            dma(line),
+            dma((count,)),
+            dma((count,)),
+            dma((reps,)),
+            dma((reps,)),
+            dma((count,)),
+            dma((count,)),
+            dma,
+        ],
+        compiler_params=pltpu.CompilerParams(
+            collective_id=3, has_side_effects=True, vmem_limit_bytes=VMEM_MOST
+        ),
+        cost_estimate=pl.CostEstimate(flops=1 << 24, bytes_accessed=1 << 26, transcendentals=0),
+    )(deltas, gains, slopes.reshape(count, tokens // count, width))
 
 
 def local(
@@ -218,54 +945,30 @@
     normed_two = (hidden_one * second_scale * gain_two).astype(low)
     local_experts = gate_weight.shape[0]
     experts = local_experts * shards
-    hidden_width = gate_weight.shape[2]
     hits = expert_ids[:, :, None] == jnp.arange(experts, dtype=jnp.int32)[None, None, :]
     mixing = jnp.sum(jnp.where(hits, gates[:, :, None], 0.0), axis=1)[unpack_order]
     mixing = lax.all_to_all(mixing.T, "shard", split_axis=0, concat_axis=0, tiled=True)
-    mixing = mixing.reshape(shards, local_experts, shards, block)
-    mixing = mixing.transpose(1, 2, 0, 3).reshape(local_experts, shards * group_count, 1)
-
-    def swap(rows):
-        return rows.reshape(shards, shards, block, width).swapaxes(0, 1).reshape(-1, width)
-
-    rows = swap(lax.all_gather(normed_two[unpack_order], "shard", axis=0, tiled=True))
-    slope_rows = all_slopes.reshape(-1, width)
-    gate_act = jnp.einsum("td,edf->etf", rows, gate_weight, preferred_element_type=full)
-    up_act = jnp.einsum("td,edf->etf", rows, up_weight, preferred_element_type=full)
-    sigmoid_gate = jax.nn.sigmoid(gate_act)
-    silu_gate = gate_act * sigmoid_gate
-    inner = (mixing * (silu_gate * up_act)).astype(low)
-    inner_slope = mixing * jnp.einsum(
-        "td,efd->etf", slope_rows, down_weight, preferred_element_type=full
-    )
-    up_slope = (inner_slope * silu_gate).astype(low)
-    gate_slope = (
-        inner_slope * up_act * sigmoid_gate * (1.0 + gate_act * (1.0 - sigmoid_gate))
-    ).astype(low)
-    delta_down = jnp.einsum("etf,td->efd", inner, slope_rows, preferred_element_type=full)
-    delta_gate = jnp.einsum("td,etf->edf", rows, gate_slope, preferred_element_type=full)
-    delta_up = jnp.einsum("td,etf->edf", rows, up_slope, preferred_element_type=full)
-    expert_deltas = lax.psum(
-        (delta_gate.astype(low), delta_up.astype(low), delta_down.astype(low)), "rep"
-    )
-    row_slopes = jnp.einsum("etf,edf->td", gate_slope, gate_weight, preferred_element_type=full)
-    row_slopes = row_slopes + jnp.einsum(
-        "etf,edf->td", up_slope, up_weight, preferred_element_type=full
-    )
-    back = lax.psum_scatter(
-        swap(row_slopes.astype(low)), "shard", scatter_dimension=0, tiled=True
-    )
-    normed_two_slope = back[pack_order].astype(full)
-    result = jnp.einsum("etf,efd->td", inner, down_weight, preferred_element_type=full)
-    shared = lax.dynamic_update_slice_in_dim(
-        jnp.zeros((shards, shards, block, width), low),
-        hidden_one.astype(low)[unpack_order].reshape(shards, 1, block, width),
-        me,
-        axis=1,
-    ).reshape(-1, width)
-    out_tokens = lax.psum_scatter(
-        (result + shared.astype(full)).astype(low), "shard", scatter_dimension=0, tiled=True
-    )
+    mixing = mixing.reshape(shards, local_experts, group_count).swapaxes(1, 2)
+    inner, row_slopes, delta_gate, delta_up, delta_down = expert_pass(
+        normed_two[unpack_order],
+        all_slopes,
+        mixing,
+        gate_weight,
+        up_weight,
+        down_weight,
+        shards,
+    )
+    expert_deltas = lax.psum((delta_gate, delta_up, delta_down), "rep")
+    back, out_tokens = return_pass(
+        row_slopes,
+        inner,
+        gate_weight,
+        up_weight,
+        down_weight,
+        hidden_one[unpack_order],
+        shards,
+    )
+    normed_two_slope = back[pack_order]
     hidden_slope, delta_second = norm_back(hidden_one, second_scale, gain_two, normed_two_slope)
     hidden_slope = slopes + hidden_slope
     attn_slope = hidden_slope.astype(low)
@@ -295,23 +998,17 @@
     )
     input_slope, delta_first = norm_back(inputs, first_scale, gain_one, normed_slope)
     input_slope = (hidden_slope + input_slope).astype(low)
-    delta_tokens = lax.all_to_all(
-        input_slope[unpack_order], "shard", split_axis=0, concat_axis=0, tiled=True
-    )
-    attention_deltas = lax.psum_scatter(
+    gain_rows = jnp.stack([delta_first, delta_second] + [jnp.zeros_like(delta_first)] * 6)
+    attention_deltas, gain_deltas, delta_tokens = settle_pass(
         jnp.concatenate([deltas.astype(low), delta_output.astype(low)], axis=1),
-        "shard",
-        scatter_dimension=0,
-        tiled=True,
-    )
-    attention_deltas = lax.psum(attention_deltas, "rep").astype(full)
-    gain_deltas = lax.psum(jnp.stack([delta_first, delta_second]), ("rep", "shard"))
-    gain_deltas = lax.dynamic_slice_in_dim(
-        gain_deltas, me * first_gain.shape[0], first_gain.shape[0], axis=1
+        gain_rows.reshape(8, shards, -1).swapaxes(0, 1),
+        input_slope[unpack_order],
+        shards,
+        lax.axis_size("rep"),
     )
     return (
         out_tokens,
-        delta_tokens,
+        delta_tokens.reshape(group_count, width),
         gain_deltas[0],
         attention_deltas[:, :query_width],
         attention_deltas[:, query_width : query_width + key_width],

time: 838 us -> 637 us (0.76)
  Pallas kernels: 0 us -> 298 us
  waiting for transfers between devices: 396 us -> 134 us
  matrix products: 216 us -> 70.2 us
  blocking collectives: 87.2 us -> 20.5 us
  local copies, waits for them, and re-layouts: 63.4 us -> 36.4 us
    pallas_call x0 -> x3, Pallas kernels: none -> 298 us  [the longest x1 115 us: return_pass(): pl.pallas_call(functools.partial(return_kernel, count), name='return_pass...]
    reduce_scatter x3 -> x0, waiting for transfers between devices: 147 us -> none  [the longest x1 67 us: local(): lax.psum_scatter(swap(row_slopes.astype(low)), 'shard', scatter_dimension...]
    dot_general x9 -> x0, matrix products: 145 us -> none  [the longest x1 29.4 us: local(): jnp.einsum('td,efd->etf', slope_rows, down_weight, preferred_element_type...]
    psum x1, waiting for transfers between devices: 162 us -> 99 us  [local(): expert_deltas = lax.psum((delta_gate, delta_up, delta_down), 'rep')]
    psum x1 -> x0, blocking collectives: 57.3 us -> none  [local(): lax.psum(jnp.stack([delta_first, delta_second]), ('rep', 'shard'))]
    all_gather x1 -> x0, waiting for transfers between devices: 44.8 us -> none  [local(): lax.all_gather(normed_two[unpack_order], 'shard', axis=0, tiled=True)]
    unnamed x123 -> x104, local copies, waits for them, and re-layouts: 17.8 us -> 5.75 us
    reshape x2 -> x0, local copies, waits for them, and re-layouts: 8.76 us -> none  [the longest x1 8.65 us: swap(): rows.reshape(shards, shards, block, width).swapaxes(0, 1).reshape(-1, width)]
  transfers between devices with their start and end apart: 9 -> 5, of which waited for: 7 -> 4; matrix products, arithmetic and copies ran while one was open for 16% -> 15% of each run, Pallas kernels for 0% -> 16%
where the time goes in v2:
time: 637 us; the launch traced here: 626 us
  Pallas kernels  298 us (47%)
  waiting for transfers between devices  134 us (21%)
  matrix products  70.2 us (11%)
  other arithmetic  43.6 us (7%)
  local copies, waits for them, and re-layouts  36.4 us (6%)
  blocking collectives  20.5 us (3%)
  between operations  15.1 us (2%)
  starting transfers between devices  8.85 us (1%)
    pallas_call x1, Pallas kernels, return_pass(): pl.pallas_call(functools.partial(return_kernel, count), name='return_pass...  115 us
    psum x1, waiting for transfers between devices, local(): expert_deltas = lax.psum((delta_gate, delta_up, delta_down), 'rep')  99 us
    pallas_call x1, Pallas kernels, settle_pass(): pl.pallas_call(functools.partial(settle_kernel, count, reps), name='settl...  97.9 us
    pallas_call x1, Pallas kernels, expert_pass(): pl.pallas_call(functools.partial(expert_kernel, count), name='expert_pass...  85.4 us
    all_gather x1, blocking collectives, local(): lax.all_gather(jnp.stack([first_gain, second_gain]), 'shard', axis=1, til...  20.5 us
    dot_general x1, matrix products, one_block(): jnp.einsum('igzd,jgd->gzij', slope_block, value_rows, preferred_element_t...  14.9 us
    all_gather x1, waiting for transfers between devices, local(): lax.all_gather(jnp.concatenate([query_weight, key_matrix, value_matrix, o...  14.8 us
    all_gather x1, waiting for transfers between devices, local(): all_slopes = lax.all_gather(cotangent, 'shard', axis=0, tiled=False)  14.7 us
  transfers between devices with their start and end apart: 5, of which 4 were waited for; matrix products, arithmetic and copies ran while one was open for 15% of the time, Pallas kernels for 16%

profile of v2, /device:TPU:0, one launch (start us, length us, event | category | flops | bytes accessed | tf_op | source)
XLA Modules:
  0.0 626.4 jit_solution(886851011947305568)
XLA Ops:
  12.2 5.2 all-to-all-start.1
  17.7 4.5 all-to-all-done.1
  22.2 3.6 all-to-all-start
  27.0 20.5 %all_gather.12 = bf16[2,1024]{1,0:T(2,128)(2,1)S(1)} all-gather(bf16[2,128]{1,0:T(2,128)(2,1)S(1)} %pad_maximum_fusion.10), channel_id=1, replica_groups=mesh['rep'=4,'shard'=8] {'shard'}, dimensions={1}, use_global_device_ids=true | all-gather | bytes 4608 | tf_op jit(solution)/shard_map/all_gather | solution.py:913
  53.0 14.8 %all-gather.4.cloned.1.call-done = bf16[1024,3072]{1,0:T(8,128)(2,1)} async-done(((bf16[128,3072]{1,0:T(8,128)(2,1)}), bf16[1024,3072]{1,0:T(8,128)(2,1)}) %all-gather.4.cloned.1.call-update) | async-done | bytes 6291472 | tf_op jit(solution)/shard_map/all_gather | solution.py:903
  70.1 3.2 fusion.21
  76.2 7.3 %fusion.60 = (f32[8,2,512]{2,1,0:T(2,128)S(1)}, f32[8,2,512,512]{2,3,1,0:T(8,128)}) fusion(bf16[512,8,2,32]{0,3,2,1:T(8,128)(2,1)S(1)} %bitcast.107, bf16[512,8,2,32]{0,3,2,1:T(8,128)(2,1)S(1)} %bitcast.105, bf16[512,8,32]{0,2,1:T(8,128)(2,1)S(1)} %get-tuple-element.102, bf16[512,8,32]{0,2,1:T(8,128)(2,1)S(1)} %get-tuple-element.101, ...), kind=kOutput, calls=%fused_computation.121 | convolution fusion | flops 552591360 | bytes 18644992 | tf_op jit(solution)/shard_map/while/body/eval_jaxpr/igzd,jgd->gzij/dot_general | solution.py:63
  83.4 8.2 %fusion.3 = f32[8,2,512]{2,1,0:T(2,128)S(1)} fusion(f32[8,2,512,512]{2,3,1,0:T(8,128)} %get-tuple-element.114, f32[8,2,512]{2,1,0:T(2,128)S(1)} %get-tuple-element.113), kind=kLoop, calls=%fused_computation.16 | loop fusion | flops 8380416 | bytes 16842752 | tf_op jit(solution)/shard_map/while/body/eval_jaxpr/reduce_sum | solution.py:88
  91.7 7.5 %fusion.29 = bf16[8,64,2,512]{3,1,2,0:T(8,128)(2,1)S(1)} fusion(bf16[512,8,64,1]{0,2,3,1:T(8,128)(2,1)S(1)} %bitcast.116, f32[8,2,512,512]{2,3,1,0:T(8,128)} %get-tuple-element.114, f32[8,2,512]{2,1,0:T(2,128)S(1)} %fusion.3, f32[8,2,512]{2,1,0:T(2,128)S(1)} %get-tuple-element.113), kind=kOutput, calls=%fused_computation.55 | convolution fusion | flops 549978112 | bytes 18415616 | tf_op jit(solution)/shard_map/while/body/eval_jaxpr/gzij,jgd->igzd/dot_general | solution.py:90
  99.2 3.4 multiply_reduce_fusion.2
  102.6 3.1 gather_fusion.3
  106.0 2.8 gather_fusion.1
  109.4 14.7 %all-gather.6.cloned.1.call-done = bf16[4096,1024]{1,0:T(8,128)(2,1)} async-done(((bf16[512,1024]{1,0:T(8,128)(2,1)}), bf16[4096,1024]{1,0:T(8,128)(2,1)}) %all-gather.6.cloned.1.call-update) | async-done | bytes 8388624 | tf_op jit(solution)/shard_map/all_gather | solution.py:916
  124.1 85.4 %expert_pass.1 = (bf16[8,512,1024]{2,1,0:T(8,128)(2,1)}, bf16[8,512,2048]{2,1,0:T(8,128)(2,1)}, bf16[2,1024,512]{2,1,0:T(8,128)(2,1)}, bf16[2,1024,512]{2,1,0:T(8,128)(2,1)}, bf16[2,512,1024]{2,1,0:T(8,128)(2,1)}) custom-call(bf16[512,1024]{1,0:T(8,128)(2,1)} %gather_fusion.1, bf16[8,8,64,1024]{3,2,1,0:T(8,128)(2,1)} %bitcast.127, f32[8,512,2]{2,1,0:T(8,128)} %bitcast.109, ...), custom_call_target="tpu_custom_call" | custom-call | flops 51539607552 | bytes 67108864 | tf_op jit(solution)/shard_map/expert_pass/pallas_call | solution.py:327
  209.5 114.7 %return_pass.1 = (f32[512,1024]{1,0:T(8,128)}, bf16[512,1024]{1,0:T(8,128)(2,1)}) custom-call(bf16[8,512,2048]{2,1,0:T(8,128)(2,1)} %get-tuple-element.72.grad_ref, bf16[8,8,64,1024]{3,2,1,0:T(8,128)(2,1)} %bitcast.144, bf16[2,1024,512]{2,1,0:T(8,128)(2,1)} %gate_ref.3, bf16[2,1024,512]{2,1,0:T(8,128)(2,1)} %up_ref.3, bf16[2,512,1024]{2,1,0:T(8,128)(2,1)} %down_ref.3, ...), custom_call_target="tpu_custom_call" | custom-call | flops 25769803776 | bytes 67108864 | tf_op jit(solution)/shard_map/return_pass/pallas_call | solution.py:528
  327.7 5.3 gather_fusion.5
  337.2 2.9 fusion.30
  341.2 14.9 %fusion = (f32[8,2,512]{2,1,0:T(2,128)S(1)}, f32[8,512,512,2]{2,1,3,0:T(8,128)}) fusion(f32[8,2,512,512]{2,3,1,0:T(8,128)} %get-tuple-element.114, f32[8,2,512]{2,1,0:T(2,128)} %bitcast.122, bf16[512,8,64,1]{0,2,3,1:T(8,128)(2,1)S(1)} %bitcast.117, bf16[512,8,2,64]{0,3,2,1:T(8,128)(2,1)S(1)} %bitcast.101), kind=kOutput, calls=%fused_computation.9 | convolution fusion | flops 549445632 | bytes 35192832 | tf_op jit(solution)/shard_map/while/body/eval_jaxpr/igzd,jgd->gzij/dot_general | solution.py:109
  356.1 10.9 %fusion.2 = bf16[8,2,512,512]{2,3,1,0:T(8,128)(2,1)} fusion(f32[8,512,512,2]{2,1,3,0:T(8,128)} %get-tuple-element.118, f32[8,2,512,512]{2,3,1,0:T(8,128)S(1)} %bitcast.96, f32[8,2,512]{2,1,0:T(2,128)S(1)} %get-tuple-element.117, f32[8,2,512]{2,1,0:T(2,128)S(1)} %bitcast.124), kind=kLoop, calls=%fused_computation.11 | loop fusion | flops 16777216 | bytes 42008576 | tf_op jit(solution)/shard_map/while/body/eval_jaxpr/convert_element_type | solution.py:113
  368.2 6.2 fusion.37
  375.4 5.3 convolution_multiply_fusion
  382.2 3.7 fusion.38
  385.9 5.6 fusion.20
  392.1 3.0 gather_fusion.6
  395.8 3.3 convolution_convert_fusion.1
  399.1 2.7 convolution_convert_fusion
  401.8 3.2 pad_maximum_fusion.delta_ref
  405.0 97.9 %settle_pass.1 = (f32[128,3072]{1,0:T(8,128)}, f32[8,128]{1,0:T(8,128)}, bf16[8,64,1024]{2,1,0:T(8,128)(2,1)}) custom-call(bf16[1024,3072]{1,0:T(8,128)(2,1)} %pad_maximum_fusion.delta_ref, f32[8,8,128]{2,1,0:T(8,128)} %maximum_bitcast_fusion.3.gain_ref, bf16[8,64,1024]{2,1,0:T(8,128)(2,1)} %bitcast.104), custom_call_target="tpu_custom_call" | custom-call | flops 16777216 | bytes 67108864 | tf_op jit(solution)/shard_map/settle_pass/pallas_call | solution.py:833
  508.4 99.0 %all-reduce.3.cloned.1.call-done = (bf16[2,1024,512]{2,1,0:T(8,128)(2,1)}, bf16[2,1024,512]{2,1,0:T(8,128)(2,1)}, bf16[2,512,1024]{2,1,0:T(8,128)(2,1)}) async-done(((bf16[2,1024,512]{2,1,0:T(8,128)(2,1)}, bf16[2,1024,512]{2,1,0:T(8,128)(2,1)}, bf16[2,512,1024]{2,1,0:T(8,128)(2,1)}), (bf16[2,1024,512]{2,1,0:T(8,128)(2,1)}, bf16[2,1024,512]{2,1,0:T(8,128)(2,1)}, ...) | async-done | bytes 6291472 | tf_op jit(solution)/shard_map/psum | solution.py:961
  607.4 4.3 convert_element_type.111
  611.8 2.6 convert_element_type.112
  614.4 2.5 convert_element_type.113
  (163 shorter events, 39.4 us)
Async XLA Ops:
  7.2 60.6 %all-gather.4.cloned.1.call-start = ((), (), s32[]{:S(2)}) async-start(), calls=%async_computation.2 | async-start | bytes 7077888 | tf_op jit(solution)/shard_map/all_gather | solution.py:903
  9.4 8.0 %copy-start.39 = (s32[1,4]{1,0:T(1,128)S(1)}, s32[1,4]{1,0:T(1,128)}, u32[]{:S(2)}) copy-start(s32[1,4]{1,0:T(1,128)} %param.18) | copy-start | bytes 52
  9.4 8.2 %copy-start.36 = (s32[512]{0:T(512)S(1)}, s32[512]{0:T(512)}, u32[]{:S(2)}) copy-start(s32[512]{0:T(512)} %param.19) | copy-start | bytes 6148
  9.4 114.7 %all-gather.6.cloned.1.call-start = ((), (), s32[]{:S(2)}) async-start(), calls=%async_computation.3 | async-start | bytes 9437184 | tf_op jit(solution)/shard_map/all_gather | solution.py:916
  10.4 15.4 %copy-start.40 = (bf16[128]{0:T(256)(128)(2,1)S(1)}, bf16[128]{0:T(256)(128)(2,1)}, u32[]{:S(2)}) copy-start(bf16[128]{0:T(256)(128)(2,1)} %param.28) | copy-start | bytes 772
  10.4 15.4 %copy-start.41 = (bf16[128]{0:T(256)(128)(2,1)S(1)}, bf16[128]{0:T(256)(128)(2,1)}, u32[]{:S(2)}) copy-start(bf16[128]{0:T(256)(128)(2,1)} %param.23) | copy-start | bytes 772
  12.2 10.0 %all-to-all-start.1 = ((f32[8,2,512]{2,1,0:T(2,128)}), f32[8,2,512]{2,1,0:T(2,128)S(1)}, u32[]{:S(2)}, u32[]{:S(2)}) async-start(f32[8,2,512]{2,1,0:T(2,128)} %all_to_all.17), calls=%async_computation.1 | async-start | bytes 65536 | tf_op jit(solution)/shard_map/all_to_all | solution.py:950
  22.2 27.9 %all-to-all-start = ((bf16[8,64,1024]{2,1,0:T(8,128)(2,1)}), bf16[8,64,1024]{2,1,0:T(8,128)(2,1)S(1)}, u32[]{:S(2)}, u32[]{:S(2)}) async-start(bf16[8,64,1024]{2,1,0:T(8,128)(2,1)} %bitcast), calls=%async_computation | async-start | bytes 2097152 | tf_op jit(solution)/shard_map/all_to_all | solution.py:898
  25.8 581.6 %all-reduce.3.cloned.1.call-start = ((), (), s32[]{:S(2)}) async-start(), calls=%async_computation.4 | async-start | bytes 12582912 | tf_op jit(solution)/shard_map/psum | solution.py:961
  47.5 26.1 %copy-start.30 = (f32[1,1024]{1,0:T(1,128)}, f32[1,1024]{1,0:T(1,128)S(1)}, u32[]{:S(2)}) copy-start(f32[1,1024]{1,0:T(1,128)S(1)} %get-tuple-element.106) | copy-start | bytes 12292
  47.9 25.4 %copy-start.13 = (f32[512,32]{0,1:T(8,128)}, f32[512,32]{0,1:T(8,128)S(1)}, u32[]{:S(2)}) copy-start(f32[512,32]{0,1:T(8,128)S(1)} %get-tuple-element.107) | copy-start | bytes 196612
  47.9 25.4 %copy-start.15 = (f32[512,32]{0,1:T(8,128)}, f32[512,32]{0,1:T(8,128)S(1)}, u32[]{:S(2)}) copy-start(f32[512,32]{0,1:T(8,128)S(1)} %get-tuple-element.108) | copy-start | bytes 196612
  52.1 47.1 %copy-start.3 = (bf16[512,1024]{1,0:T(8,128)(2,1)}, bf16[512,1024]{1,0:T(8,128)(2,1)S(1)}, u32[]{:S(2)}) copy-start(bf16[512,1024]{1,0:T(8,128)(2,1)S(1)} %gather_fusion) | copy-start | bytes 3145732
  53.0 20.6 %copy-start.32 = (f32[512]{0:T(512)}, f32[512]{0:T(512)S(1)}, u32[]{:S(2)}) copy-start(f32[512]{0:T(512)S(1)} %get-tuple-element.110) | copy-start | bytes 6148
  70.0 6.1 copy-start.20
  70.1 6.1 copy-start.22
  76.1 15.5 %copy-start.24 = (bf16[512,512]{0,1:T(8,128)(2,1)}, bf16[512,512]{0,1:T(8,128)(2,1)S(1)}, u32[]{:S(2)}) copy-start(bf16[512,512]{0,1:T(8,128)(2,1)S(1)} %convolution_convert_fusion.2) | copy-start | bytes 1572868
  340.7 15.4 %slice-start = ((s8[16777216]{0:T(1024)(128)(4,1)}), s8[4194304]{0:T(1024)(128)(4,1)S(1)}, s32[]{:S(2)}) async-start(s8[16777216]{0:T(1024)(128)(4,1)} %bitcast.95), calls=%async_computation.5 | async-start | bytes 8388608
  341.2 14.9 %slice-start.1 = ((s8[16777216]{0:T(1024)(128)(4,1)}), s8[4194304]{0:T(1024)(128)(4,1)S(1)}, s32[]{:S(2)}) async-start(s8[16777216]{0:T(1024)(128)(4,1)} %bitcast.95), calls=%async_computation.6 | async-start | bytes 8388608
  341.2 14.9 %slice-start.2 = ((s8[16777216]{0:T(1024)(128)(4,1)}), s8[4194304]{0:T(1024)(128)(4,1)S(1)}, s32[]{:S(2)}) async-start(s8[16777216]{0:T(1024)(128)(4,1)} %bitcast.95), calls=%async_computation.7 | async-start | bytes 8388608
  341.2 14.9 %slice-start.3 = ((s8[16777216]{0:T(1024)(128)(4,1)}), s8[4194304]{0:T(1024)(128)(4,1)S(1)}, s32[]{:S(2)}) async-start(s8[16777216]{0:T(1024)(128)(4,1)} %bitcast.95), calls=%async_computation.8 | async-start | bytes 8388608
  341.2 14.9 %copy-start.27 = (f32[2,8,512]{2,1,0:T(8,128)S(1)}, f32[2,8,512]{2,1,0:T(8,128)}, u32[]{:S(2)}) copy-start(f32[2,8,512]{2,1,0:T(8,128)} %log_add_fusion) | copy-start | bytes 98308
  368.2 6.2 copy-start.14
  368.2 6.2 copy-start.16
  368.2 7.2 %copy-start.21 = (bf16[512,8,32]{0,2,1:T(8,128)(2,1)S(1)}, bf16[512,8,32]{0,2,1:T(8,128)(2,1)}, u32[]{:S(2)}) copy-start(bf16[512,8,32]{0,2,1:T(8,128)(2,1)} %copy-done.20) | copy-start | bytes 786436
  368.2 7.2 %copy-start.23 = (bf16[512,8,32]{0,2,1:T(8,128)(2,1)S(1)}, bf16[512,8,32]{0,2,1:T(8,128)(2,1)}, u32[]{:S(2)}) copy-start(bf16[512,8,32]{0,2,1:T(8,128)(2,1)} %copy-done.22) | copy-start | bytes 786436
  368.2 13.9 %slice-start.4 = ((s8[16777216]{0:T(1024)(128)(4,1)}), s8[4194304]{0:T(1024)(128)(4,1)S(1)}, s32[]{:S(2)}) async-start(s8[16777216]{0:T(1024)(128)(4,1)} %bitcast.97), calls=%async_computation.9 | async-start | bytes 8388608
  368.2 13.9 %slice-start.5 = ((s8[16777216]{0:T(1024)(128)(4,1)}), s8[4194304]{0:T(1024)(128)(4,1)S(1)}, s32[]{:S(2)}) async-start(s8[16777216]{0:T(1024)(128)(4,1)} %bitcast.97), calls=%async_computation.10 | async-start | bytes 8388608
  374.4 7.7 %slice-start.6 = ((s8[16777216]{0:T(1024)(128)(4,1)}), s8[4194304]{0:T(1024)(128)(4,1)S(1)}, s32[]{:S(2)}) async-start(s8[16777216]{0:T(1024)(128)(4,1)} %bitcast.97), calls=%async_computation.11 | async-start | bytes 8388608
  375.4 6.7 %slice-start.7 = ((s8[16777216]{0:T(1024)(128)(4,1)}), s8[4194304]{0:T(1024)(128)(4,1)S(1)}, s32[]{:S(2)}) async-start(s8[16777216]{0:T(1024)(128)(4,1)} %bitcast.97), calls=%async_computation.12 | async-start | bytes 8388608
  385.9 5.6 copy-start.6
  385.9 5.6 copy-start.34
  (24 other events, 67.7 us)
Sparse Core Ops, SparseCore 0:
  10.5 57.2 all-gather.3
  69.7 54.3 all-gather.5
  367.1 240.2 all-reduce.2

commit v3 on v2

--- a/solution.py
+++ b/solution.py
@@ -23,28 +23,6 @@
     return (jnp.cos(angle), jnp.sin(angle))
 
 
-def rotary_apply(heads, cosine_table, sine_table):
-    half = heads.shape[-1] // 2
-    first = heads[..., :half]
-    second = heads[..., half:]
-    along = cosine_table[:, None, :]
-    across = sine_table[:, None, :]
-    return jnp.concatenate(
-        [first * along - second * across, second * along + first * across], axis=-1
-    )
-
-
-def rotary_inverse(heads, cosine_table, sine_table):
-    half = heads.shape[-1] // 2
-    first = heads[..., :half]
-    second = heads[..., half:]
-    along = cosine_table[:, None, :]
-    across = sine_table[:, None, :]
-    return jnp.concatenate(
-        [first * along + second * across, second * along - first * across], axis=-1
-    )
-
-
 def segment_info(lengths, group_count):
     ends = jnp.cumsum(lengths)
     starts = ends - lengths
@@ -56,96 +34,6 @@
     offset = jnp.sum(inside * starts[None, :], axis=1)
     return (segment, place - offset)
 
-
-def masked_scores(query_block, key_rows, start, segment, scale):
-    width = query_block.shape[0]
-    scores = (
-        jnp.einsum("igzd,jgd->gzij", query_block, key_rows, preferred_element_type=jnp.float32)
-        * scale
-    )
-    rows = start + jnp.arange(width, dtype=jnp.int32)
-    columns = jnp.arange(key_rows.shape[0], dtype=jnp.int32)
-    allowed = (segment[:, None] == segment[None, :]) & (columns[None, :] <= rows[:, None])
-    return jnp.where(allowed, scores, -1e30)
-
-
-def block_starts(group_count):
-    width = min(512, group_count)
-    blocks = group_count // width
-    return (width, blocks, jnp.arange(blocks, dtype=jnp.int32) * width)
-
-
-def attend(query_rows, key_rows, value_rows, segment, scale):
-    group_count = query_rows.shape[0]
-    width, blocks, starts = block_starts(group_count)
-    grouped = query_rows.reshape((blocks, width) + query_rows.shape[1:])
-
-    def one_block(piece):
-        query_block, start = piece
-        scores = masked_scores(query_block, key_rows, start, segment, scale)
-        largest = jnp.max(scores, axis=-1, keepdims=True)
-        powers = jnp.exp(scores - largest)
-        totals = jnp.sum(powers, axis=-1, keepdims=True)
-        weights = (powers / totals).astype(jnp.bfloat16)
-        mixed = jnp.einsum(
-            "gzij,jgd->igzd", weights, value_rows, preferred_element_type=jnp.float32
-        )
-        return (mixed.astype(jnp.bfloat16), (largest + jnp.log(totals))[..., 0])
-
-    mixed, logsum = lax.map(one_block, (grouped, starts))
-    return (mixed.reshape(group_count, -1), logsum)
-
-
-def attend_back(query_rows, key_rows, value_rows, segment, scale, logsum, mixed_slope):
-    group_count = query_rows.shape[0]
-    width, blocks, starts = block_starts(group_count)
-    grouped = query_rows.reshape((blocks, width) + query_rows.shape[1:])
-    slope_blocks = mixed_slope.reshape(grouped.shape)
-
-    def one_block(piece):
-        query_block, slope_block, logsum_block, start = piece
-        scores = masked_scores(query_block, key_rows, start, segment, scale)
-        probs = jnp.exp(scores - logsum_block[..., None])
-        prob_slope = jnp.einsum(
-            "igzd,jgd->gzij", slope_block, value_rows, preferred_element_type=jnp.float32
-        )
-        inner = jnp.sum(probs * prob_slope, axis=-1, keepdims=True)
-        score_slope = (probs * (prob_slope - inner)).astype(jnp.bfloat16)
-        query_slope = (
-            jnp.einsum("gzij,jgd->igzd", score_slope, key_rows, preferred_element_type=jnp.float32)
-            * scale
-        )
-        key_gradient = (
-            jnp.einsum(
-                "gzij,igzd->jgd", score_slope, query_block, preferred_element_type=jnp.float32
-            )
-            * scale
-        )
-        value_gradient = jnp.einsum(
-            "gzij,igzd->jgd",
-            probs.astype(jnp.bfloat16),
-            slope_block,
-            preferred_element_type=jnp.float32,
-        )
-        return (query_slope, key_gradient, value_gradient)
-
-    query_slope, key_gradient, value_gradient = lax.map(
-        one_block, (grouped, slope_blocks, logsum, starts)
-    )
-    return (
-        query_slope.reshape(group_count, -1, query_rows.shape[-1]),
-        jnp.sum(key_gradient, axis=0),
-        jnp.sum(value_gradient, axis=0),
-    )
-
-
-def norm_back(inputs, scale_rows, gain, slope):
-    scaled = slope * gain
-    gain_slope = jnp.sum(slope * inputs * scale_rows, axis=0)
-    input_slope = scale_rows * scaled - inputs * scale_rows**3 * jnp.mean(
-        inputs * scaled, axis=1, keepdims=True
-    )
-    return (input_slope, gain_slope)
 
 MESH = pl.DeviceIdType.MESH
 NN = (((1,), (0,)), ((), ()))
@@ -507,7 +395,7 @@
         total[...] = value
         mine = pl.ds(pl.multiple_of(me * block, block), block)
         theirs = pl.ds(pl.multiple_of(pack * block, block), block)
-        total[mine, :] += own_ref[theirs, :]
+        total[mine, :] += own_ref[theirs, :].astype(jnp.float32)
         return total[...]
 
     reduce(0, grad_load, grad_part, 0)
@@ -871,6 +759,344 @@
     )(deltas, gains, slopes.reshape(count, tokens // count, width))
 
 
+def turn_pairs(rows, along, across, sign):
+    lane = lax.broadcasted_iota(jnp.int32, (rows.shape[0], 128), 1)
+    early = (lane % HEAD_SIZE) < HEAD_SIZE // 2
+    pieces = []
+    for at in range(0, rows.shape[1], 128):
+        part = rows[:, at : at + 128]
+        other = jnp.where(
+            early,
+            pltpu.roll(part, 128 - HEAD_SIZE // 2, 1),
+            pltpu.roll(part, HEAD_SIZE // 2, 1),
+        )
+        pieces.append(part * along + sign * (other * across))
+    return pieces[0] if len(pieces) == 1 else jnp.concatenate(pieces, axis=1)
+
+
+def permutation(order_ref):
+    tokens = order_ref.shape[0]
+    columns = lax.broadcasted_iota(jnp.int32, (tokens, tokens), 1)
+    return jnp.where(order_ref[...] == columns, 1.0, 0.0).astype(jnp.bfloat16)
+
+
+def fill_bias(bias, row_ref, column_ref):
+    tokens = bias.shape[0]
+    keys = lax.broadcasted_iota(jnp.int32, (tokens, tokens), 0)
+    queries = lax.broadcasted_iota(jnp.int32, (tokens, tokens), 1)
+    allowed = (column_ref[...] == row_ref[...]) & (keys <= queries)
+    bias[...] = jnp.where(allowed, 0.0, -1e30)
+
+
+def query_spans(tokens):
+    half = tokens // 2
+    return ((0, half, half), (half, half, tokens))
+
+
+def attention_kernel(
+    arrived_ref,
+    order_ref,
+    row_ref,
+    column_ref,
+    along_ref,
+    across_ref,
+    weight_ref,
+    gain_ref,
+    input_out,
+    query_out,
+    key_out,
+    value_out,
+    mixed_out,
+    logsum_out,
+    hidden_out,
+    normed_out,
+    shared_out,
+    place,
+    bias,
+    normed,
+):
+    low = jnp.bfloat16
+    full = jnp.float32
+    tokens, width = arrived_ref.shape
+    key_width = key_out.shape[1]
+    place[...] = permutation(order_ref)
+    inputs = matmul(place[...], arrived_ref[...], NN)
+    input_out[...] = inputs.astype(low)
+    scale = lax.rsqrt(jnp.mean(inputs * inputs, axis=1, keepdims=True) + EPS)
+    normed[...] = (inputs * scale * gain_ref[0:1, :]).astype(low)
+    fill_bias(bias, row_ref, column_ref)
+    along = along_ref[...]
+    across = across_ref[...]
+    for at in range(0, width, 512):
+        part = matmul(normed[...], weight_ref[:, at : at + 512], NN)
+        query_out[:, at : at + 512] = turn_pairs(part, along, across, 1.0).astype(low)
+    part = matmul(normed[...], weight_ref[:, width : width + key_width], NN)
+    key_out[...] = turn_pairs(part, along, across, 1.0).astype(low)
+    part = matmul(normed[...], weight_ref[:, width + key_width : width + 2 * key_width], NN)
+    value_out[...] = part.astype(low)
+
+    def heads(g, carry):
+        kv = pl.ds(pl.multiple_of(g * 128, 128), 128)
+        qs = pl.ds(pl.multiple_of(g * 256, 256), 256)
+        keys = key_out[:, kv]
+        values = value_out[:, kv]
+        queries = query_out[:, qs] * jnp.bfloat16(HEAD_SIZE**-0.5)
+        for start, size, reach in query_spans(tokens):
+            pieces = []
+            for h in range(4):
+                a = (h // 2) * HEAD_SIZE
+                score = matmul(
+                    keys[:reach, a : a + HEAD_SIZE],
+                    queries[start : start + size, h * HEAD_SIZE : (h + 1) * HEAD_SIZE],
+                    NT,
+                )
+                score = score + bias[:reach, start : start + size]
+                largest = jnp.max(score, axis=0, keepdims=True)
+                powers = jnp.exp(score - largest)
+                totals = jnp.sum(powers, axis=0, keepdims=True)
+                weights = (powers * (1.0 / totals)).astype(low)
+                pieces.append(matmul(weights, values[:reach, a : a + HEAD_SIZE], TN))
+                logsum_out[g, h : h + 1, start : start + size] = largest + jnp.log(totals)
+            mixed_out[start : start + size, qs] = jnp.concatenate(pieces, axis=1).astype(low)
+        return carry
+
+    lax.fori_loop(0, key_width // 128, heads, 0)
+    hidden = input_out[...].astype(full) + matmul(
+        mixed_out[...], weight_ref[:, width + 2 * key_width :], NN
+    )
+    hidden_out[...] = hidden
+    scale = lax.rsqrt(jnp.mean(hidden * hidden, axis=1, keepdims=True) + EPS)
+    normed[...] = (hidden * scale * gain_ref[1:2, :]).astype(low)
+    normed_out[...] = matmul(place[...], normed[...], TN).astype(low)
+    shared_out[...] = matmul(place[...], hidden_out[...].astype(low), TN).astype(low)
+
+
+def attention_pass(arrived, order, row, column, along, across, weights, gains):
+    tokens, width = arrived.shape
+    key_width = (weights.shape[1] - 2 * width) // 2
+    low = jnp.bfloat16
+    full = jnp.float32
+    inside = pl.BlockSpec(memory_space=pltpu.VMEM)
+    shape = jax.ShapeDtypeStruct
+    return pl.pallas_call(
+        attention_kernel,
+        name="attention_pass",
+        out_shape=(
+            shape((tokens, width), low),
+            shape((tokens, width), low),
+            shape((tokens, key_width), low),
+            shape((tokens, key_width), low),
+            shape((tokens, width), low),
+            shape((key_width // 128, 4, tokens), full),
+            shape((tokens, width), full),
+            shape((tokens, width), low),
+            shape((tokens, width), low),
+        ),
+        in_specs=[inside] * 8,
+        out_specs=(inside,) * 9,
+        scratch_shapes=[
+            pltpu.VMEM((tokens, tokens), low),
+            pltpu.VMEM((tokens, tokens), full),
+            pltpu.VMEM((tokens, width), low),
+        ],
+        compiler_params=pltpu.CompilerParams(vmem_limit_bytes=VMEM_MOST),
+        cost_estimate=pl.CostEstimate(
+            flops=12 << 30, bytes_accessed=1 << 24, transcendentals=1 << 22
+        ),
+    )(arrived, order, row, column, along, across, weights, gains)
+
+
+def slope_kernel(
+    back_ref,
+    arrived_ref,
+    order_ref,
+    row_ref,
+    column_ref,
+    along_ref,
+    across_ref,
+    weight_ref,
+    gain_ref,
+    input_ref,
+    query_ref,
+    key_ref,
+    value_ref,
+    mixed_ref,
+    logsum_ref,
+    hidden_ref,
+    delta_out,
+    gain_out,
+    slope_out,
+    place,
+    bias,
+    normed,
+    steep,
+    mixed_slope,
+    backs,
+):
+    low = jnp.bfloat16
+    full = jnp.float32
+    tokens, width = back_ref.shape
+    key_width = key_ref.shape[1]
+    place[...] = permutation(order_ref)
+    fill_bias(bias, row_ref, column_ref)
+    high = back_ref[...].astype(low)
+    rest = (back_ref[...] - high.astype(full)).astype(low)
+    slope = matmul(place[...], high, NN) + matmul(place[...], rest, NN)
+    hidden = hidden_ref[...]
+    scale = lax.rsqrt(jnp.mean(hidden * hidden, axis=1, keepdims=True) + EPS)
+    scaled = slope * gain_ref[1:2, :]
+    gain_out[1:2, :] = jnp.sum(slope * hidden * scale, axis=0, keepdims=True)
+    steep[...] = (
+        matmul(place[...], arrived_ref[...], NN)
+        + scale * scaled
+        - hidden * (scale * scale * scale) * jnp.mean(hidden * scaled, axis=1, keepdims=True)
+    )
+    sharp = steep[...].astype(low)
+    joined = width + 2 * key_width
+    for at in range(0, width, 512):
+        delta_out[:, joined + at : joined + at + 512] = matmul(
+            mixed_ref[...], sharp[:, at : at + 512], TN
+        ).astype(low)
+    mixed_slope[...] = matmul(sharp, weight_ref[:, joined:], NT).astype(low)
+    along = along_ref[...]
+    across = across_ref[...]
+
+    def heads(g, carry):
+        kv = pl.ds(pl.multiple_of(g * 128, 128), 128)
+        qs = pl.ds(pl.multiple_of(g * 256, 256), 256)
+        keys = key_ref[:, kv]
+        values = value_ref[:, kv]
+        queries = query_ref[:, qs] * jnp.bfloat16(HEAD_SIZE**-0.5)
+        slopes = mixed_slope[:, qs]
+        key_parts = []
+        value_parts = []
+        query_parts = [[], []]
+        for a in range(2):
+            key_h = keys[:, a * HEAD_SIZE : (a + 1) * HEAD_SIZE]
+            value_h = values[:, a * HEAD_SIZE : (a + 1) * HEAD_SIZE]
+            key_slope = [None, None]
+            value_slope = [None, None]
+            for b in range(2):
+                h = 2 * a + b
+                columns = slice(h * HEAD_SIZE, (h + 1) * HEAD_SIZE)
+                for i, (start, size, reach) in enumerate(query_spans(tokens)):
+                    q = queries[start : start + size, columns]
+                    d = slopes[start : start + size, columns]
+                    score = matmul(key_h[:reach], q, NT) + bias[:reach, start : start + size]
+                    probs = jnp.exp(score - logsum_ref[g, h : h + 1, start : start + size])
+                    prob_slope = matmul(value_h[:reach], d, NT)
+                    inner = jnp.sum(probs * prob_slope, axis=0, keepdims=True)
+                    score_slope = (probs * (prob_slope - inner)).astype(low)
+                    term = matmul(probs.astype(low), d, NN)
+                    value_slope[i] = term if b == 0 else value_slope[i] + term
+                    term = matmul(score_slope, q, NN)
+                    key_slope[i] = term if b == 0 else key_slope[i] + term
+                    query_parts[i].append(matmul(score_slope, key_h[:reach], TN))
+            half = tokens // 2
+            key_parts.append(
+                jnp.concatenate([key_slope[0] + key_slope[1][:half], key_slope[1][half:]], axis=0)
+            )
+            value_parts.append(
+                jnp.concatenate(
+                    [value_slope[0] + value_slope[1][:half], value_slope[1][half:]], axis=0
+                )
+            )
+        for i, (start, size, reach) in enumerate(query_spans(tokens)):
+            rows = slice(start, start + size)
+            part = jnp.concatenate(query_parts[i], axis=1) * HEAD_SIZE**-0.5
+            backs[rows, qs] = turn_pairs(part, along[rows], across[rows], -1.0).astype(low)
+        part = jnp.concatenate(key_parts, axis=1)
+        spot = pl.ds(pl.multiple_of(width + g * 128, 128), 128)
+        backs[:, spot] = turn_pairs(part, along, across, -1.0).astype(low)
+        part = jnp.concatenate(value_parts, axis=1)
+        spot = pl.ds(pl.multiple_of(width + key_width + g * 128, 128), 128)
+        backs[:, spot] = part.astype(low)
+        return carry
+
+    lax.fori_loop(0, key_width // 128, heads, 0)
+    inputs = input_ref[...].astype(full)
+    scale = lax.rsqrt(jnp.mean(inputs * inputs, axis=1, keepdims=True) + EPS)
+    normed[...] = (inputs * scale * gain_ref[0:1, :]).astype(low)
+    for at in range(0, joined, 512):
+        delta_out[:, at : at + 512] = matmul(normed[...], backs[:, at : at + 512], TN).astype(low)
+    slope = matmul(backs[...], weight_ref[:, :joined], NT)
+    scaled = slope * gain_ref[0:1, :]
+    gain_out[0:1, :] = jnp.sum(slope * inputs * scale, axis=0, keepdims=True)
+    result = (
+        steep[...]
+        + scale * scaled
+        - inputs * (scale * scale * scale) * jnp.mean(inputs * scaled, axis=1, keepdims=True)
+    )
+    slope_out[...] = matmul(place[...], result.astype(low), TN).astype(low)
+    gain_out[2:8, :] = jnp.zeros((6, width), full)
+
+
+def slope_pass(
+    back,
+    arrived,
+    order,
+    row,
+    column,
+    along,
+    across,
+    weights,
+    gains,
+    inputs,
+    queries,
+    keys,
+    values,
+    mixed,
+    logsum,
+    hidden,
+):
+    tokens, width = back.shape
+    key_width = keys.shape[1]
+    low = jnp.bfloat16
+    full = jnp.float32
+    inside = pl.BlockSpec(memory_space=pltpu.VMEM)
+    shape = jax.ShapeDtypeStruct
+    return pl.pallas_call(
+        slope_kernel,
+        name="slope_pass",
+        out_shape=(
+            shape(weights.shape, low),
+            shape((8, width), full),
+            shape((tokens, width), low),
+        ),
+        in_specs=[inside] * 16,
+        out_specs=(inside,) * 3,
+        scratch_shapes=[
+            pltpu.VMEM((tokens, tokens), low),
+            pltpu.VMEM((tokens, tokens), full),
+            pltpu.VMEM((tokens, width), low),
+            pltpu.VMEM((tokens, width), full),
+            pltpu.VMEM((tokens, width), low),
+            pltpu.VMEM((tokens, width + 2 * key_width), low),
+        ],
+        compiler_params=pltpu.CompilerParams(vmem_limit_bytes=VMEM_MOST),
+        cost_estimate=pl.CostEstimate(
+            flops=24 << 30, bytes_accessed=1 << 24, transcendentals=1 << 22
+        ),
+    )(
+        back,
+        arrived,
+        order,
+        row,
+        column,
+        along,
+        across,
+        weights,
+        gains,
+        inputs,
+        queries,
+        keys,
+        values,
+        mixed,
+        logsum,
+        hidden,
+    )
+
+
 def local(
     tokens,
     cotangent,
@@ -893,116 +1119,52 @@
     me = lax.axis_index("shard")
     group_count, width = tokens.shape
     block = group_count // shards
-    low = jnp.bfloat16
     full = jnp.float32
     arrived = lax.all_to_all(tokens, "shard", split_axis=0, concat_axis=0, tiled=True)
-    inputs_low = arrived[pack_order]
-    inputs = inputs_low.astype(full)
     query_width = query_weight.shape[1]
     key_width = key_matrix.shape[1]
+    inputs_width = query_width + 2 * key_width
     joined = lax.all_gather(
         jnp.concatenate([query_weight, key_matrix, value_matrix, output_weight], axis=1),
         "shard",
         axis=0,
         tiled=True,
     )
-    full_query = joined[:, :query_width]
-    full_key = joined[:, query_width : query_width + key_width]
-    full_value = joined[:, query_width + key_width : query_width + 2 * key_width]
-    full_output = joined[:, query_width + 2 * key_width :]
     gains = lax.all_gather(jnp.stack([first_gain, second_gain]), "shard", axis=1, tiled=True)
-    gain_one = gains[0].astype(full)
-    gain_two = gains[1].astype(full)
+    gains = gains.astype(full)
     all_slopes = lax.all_gather(cotangent, "shard", axis=0, tiled=False)
     slope_arrived = lax.dynamic_slice_in_dim(all_slopes, me * block, block, axis=1).reshape(
         group_count, width
     )
-    slope_low = slope_arrived[pack_order]
-    slopes = slope_low.astype(full)
     segment, place = segment_info(seq_lengths[0], group_count)
     cosine_table, sine_table = rope_tables(place, HEAD_SIZE)
-    scale = HEAD_SIZE ** (-0.5)
-    head_groups = QUERY_HEADS // KEY_VALUE_HEADS
-    first_scale = lax.rsqrt(jnp.mean(inputs * inputs, axis=1, keepdims=True) + EPS)
-    normed = (inputs * first_scale * gain_one).astype(low)
-    query_projected = jnp.dot(normed, full_query, preferred_element_type=full)
-    key_projected = jnp.dot(normed, full_key, preferred_element_type=full)
-    value_projected = jnp.dot(normed, full_value, preferred_element_type=full)
-    query_rows = (
-        rotary_apply(
-            query_projected.reshape(group_count, QUERY_HEADS, HEAD_SIZE), cosine_table, sine_table
-        )
-        .astype(low)
-        .reshape(group_count, KEY_VALUE_HEADS, head_groups, HEAD_SIZE)
-    )
-    key_rows = rotary_apply(
-        key_projected.reshape(group_count, KEY_VALUE_HEADS, HEAD_SIZE), cosine_table, sine_table
-    ).astype(low)
-    value_rows = value_projected.astype(low).reshape(group_count, KEY_VALUE_HEADS, HEAD_SIZE)
-    mixed, logsum = attend(query_rows, key_rows, value_rows, segment, scale)
-    hidden_one = inputs + jnp.dot(mixed, full_output, preferred_element_type=full)
-    second_scale = lax.rsqrt(jnp.mean(hidden_one * hidden_one, axis=1, keepdims=True) + EPS)
-    normed_two = (hidden_one * second_scale * gain_two).astype(low)
+    along = jnp.concatenate([cosine_table] * 4, axis=1)
+    across = jnp.concatenate([-sine_table, sine_table] * 2, axis=1)
+    order = pack_order[:, None]
     local_experts = gate_weight.shape[0]
     experts = local_experts * shards
     hits = expert_ids[:, :, None] == jnp.arange(experts, dtype=jnp.int32)[None, None, :]
     mixing = jnp.sum(jnp.where(hits, gates[:, :, None], 0.0), axis=1)[unpack_order]
     mixing = lax.all_to_all(mixing.T, "shard", split_axis=0, concat_axis=0, tiled=True)
     mixing = mixing.reshape(shards, local_experts, group_count).swapaxes(1, 2)
+    tables = (order, segment[None, :], segment[:, None], along, across, joined, gains)
+    inputs, queries, keys, values, mixed, logsum, hidden, normed, shared = attention_pass(
+        arrived, *tables
+    )
     inner, row_slopes, delta_gate, delta_up, delta_down = expert_pass(
-        normed_two[unpack_order],
-        all_slopes,
-        mixing,
-        gate_weight,
-        up_weight,
-        down_weight,
-        shards,
+        normed, all_slopes, mixing, gate_weight, up_weight, down_weight, shards
     )
     expert_deltas = lax.psum((delta_gate, delta_up, delta_down), "rep")
     back, out_tokens = return_pass(
-        row_slopes,
-        inner,
-        gate_weight,
-        up_weight,
-        down_weight,
-        hidden_one[unpack_order],
-        shards,
-    )
-    normed_two_slope = back[pack_order]
-    hidden_slope, delta_second = norm_back(hidden_one, second_scale, gain_two, normed_two_slope)
-    hidden_slope = slopes + hidden_slope
-    attn_slope = hidden_slope.astype(low)
-    delta_output = jnp.einsum("ta,td->ad", mixed, attn_slope, preferred_element_type=full)
-    mixed_slope = jnp.einsum(
-        "td,ad->ta", attn_slope, full_output, preferred_element_type=full
-    ).astype(low)
-    query_slope, key_gradient, value_gradient = attend_back(
-        query_rows, key_rows, value_rows, segment, scale, logsum, mixed_slope
-    )
-    query_back = (
-        rotary_inverse(query_slope, cosine_table, sine_table)
-        .reshape(group_count, QUERY_HEADS * HEAD_SIZE)
-        .astype(low)
-    )
-    key_back = (
-        rotary_inverse(key_gradient, cosine_table, sine_table)
-        .reshape(group_count, KEY_VALUE_HEADS * HEAD_SIZE)
-        .astype(low)
-    )
-    value_back = value_gradient.reshape(group_count, KEY_VALUE_HEADS * HEAD_SIZE).astype(low)
-    backs = jnp.concatenate([query_back, key_back, value_back], axis=1)
-    inputs_width = backs.shape[1]
-    deltas = jnp.einsum("td,ta->da", normed, backs, preferred_element_type=full)
-    normed_slope = jnp.einsum(
-        "ta,da->td", backs, joined[:, :inputs_width], preferred_element_type=full
-    )
-    input_slope, delta_first = norm_back(inputs, first_scale, gain_one, normed_slope)
-    input_slope = (hidden_slope + input_slope).astype(low)
-    gain_rows = jnp.stack([delta_first, delta_second] + [jnp.zeros_like(delta_first)] * 6)
+        row_slopes, inner, gate_weight, up_weight, down_weight, shared, shards
+    )
+    deltas, gain_rows, slope_rows = slope_pass(
+        back, slope_arrived, *tables, inputs, queries, keys, values, mixed, logsum, hidden
+    )
     attention_deltas, gain_deltas, delta_tokens = settle_pass(
-        jnp.concatenate([deltas.astype(low), delta_output.astype(low)], axis=1),
+        deltas,
         gain_rows.reshape(8, shards, -1).swapaxes(0, 1),
-        input_slope[unpack_order],
+        slope_rows,
         shards,
         lax.axis_size("rep"),
     )

time: 637 us -> 488 us (0.77)
  waiting for transfers between devices: 134 us -> 57.2 us
  matrix products: 70.2 us -> 0 us
  Pallas kernels: 298 us -> 351 us
  other arithmetic: 43.6 us -> 14.8 us
  local copies, waits for them, and re-layouts: 36.4 us -> 15.9 us
    psum x1, waiting for transfers between devices: 99 us -> 0.01 us  [local(): expert_deltas = lax.psum((delta_gate, delta_up, delta_down), 'rep')]
    dot_general x14 -> x0, matrix products: 70.2 us -> none  [the longest x1 14.9 us: one_block(): jnp.einsum('igzd,jgd->gzij', slope_block, value_rows, preferred_element_t...]
    pallas_call x0 -> x2, Pallas kernels: none -> 53.5 us  [the longest x1 35.2 us: slope_pass(): pl.pallas_call(slope_kernel, name='slope_pass', out_shape=(shape(weights....]
    all_gather x1, waiting for transfers between devices: 14.7 us -> 38.1 us  [local(): all_slopes = lax.all_gather(cotangent, 'shard', axis=0, tiled=False)]
    gather x6 -> x0, local copies, waits for them, and re-layouts: 18.3 us -> none  [the longest x1 5.34 us: local(): normed_two_slope = back[pack_order]]
    convert_element_type x3 -> x1, other arithmetic: 11.7 us -> 0.61 us  [local(): gains = gains.astype(full)]
    reduce_sum x3 -> x0, other arithmetic: 10.8 us -> none  [the longest x1 8.19 us: one_block(): totals = jnp.sum(powers, axis=-1, keepdims=True)]
  transfers between devices with their start and end apart: 5 -> 5, of which waited for: 4 -> 3; matrix products, arithmetic and copies ran while one was open for 15% -> 3% of each run, Pallas kernels for 16% -> 55%
where the time goes in v3:
time: 488 us; the launch traced here: 483 us
  Pallas kernels  351 us (72%)
  waiting for transfers between devices  57.2 us (12%)
  blocking collectives  20.1 us (4%)
  local copies, waits for them, and re-layouts  15.9 us (3%)
  other arithmetic  14.8 us (3%)
  between operations  14.4 us (3%)
  starting transfers between devices  9.54 us (2%)
    pallas_call x1, Pallas kernels, return_pass(): pl.pallas_call(functools.partial(return_kernel, count), name='return_pass...  115 us
    pallas_call x1, Pallas kernels, settle_pass(): pl.pallas_call(functools.partial(settle_kernel, count, reps), name='settl...  97 us
    pallas_call x1, Pallas kernels, expert_pass(): pl.pallas_call(functools.partial(expert_kernel, count), name='expert_pass...  85.6 us
    all_gather x1, waiting for transfers between devices, local(): all_slopes = lax.all_gather(cotangent, 'shard', axis=0, tiled=False)  38.1 us
    pallas_call x1, Pallas kernels, slope_pass(): pl.pallas_call(slope_kernel, name='slope_pass', out_shape=(shape(weights....  35.2 us
    all_gather x1, blocking collectives, local(): lax.all_gather(jnp.stack([first_gain, second_gain]), 'shard', axis=1, til...  20.1 us
    pallas_call x1, Pallas kernels, attention_pass(): pl.pallas_call(attention_kernel, name='attention_pass', out_shape=(shape(...  18.3 us
    all_gather x1, waiting for transfers between devices, local(): lax.all_gather(jnp.concatenate([query_weight, key_matrix, value_matrix, o...  14.7 us
  transfers between devices with their start and end apart: 5, of which 3 were waited for; matrix products, arithmetic and copies ran while one was open for 3% of the time, Pallas kernels for 55%

profile of v3, /device:TPU:0, one launch (start us, length us, event | category | flops | bytes accessed | tf_op | source)
XLA Modules:
  0.0 482.9 jit_solution(10101448314968852666)
XLA Ops:
  7.3 2.1 pad_maximum_fusion
  9.4 0.7 all-gather.6.cloned.1.call-update
  10.4 1.0 gather_fusion
  11.5 0.6 all_to_all.16
  12.2 5.2 %all-to-all-start.1 = ((f32[8,2,512]{2,1,0:T(2,128)}), f32[8,2,512]{2,1,0:T(2,128)S(1)}, u32[]{:S(2)}, u32[]{:S(2)}) async-start(f32[8,2,512]{2,1,0:T(2,128)} %all_to_all.16), calls=%async_computation.1 | async-start | bytes 65536 | tf_op jit(solution)/shard_map/all_to_all | solution.py:1148
  17.4 0.2 reduce-window.4
  17.6 0.9 copy.53.order_ref
  18.4 3.8 all-to-all-done.1
  22.2 4.2 all-to-all-start
  26.6 0.9 copy.54.column_ref
  27.5 20.1 %all_gather.13 = bf16[2,1024]{1,0:T(2,128)(2,1)S(1)} all-gather(bf16[2,128]{1,0:T(2,128)(2,1)S(1)} %pad_maximum_fusion.3), channel_id=1, replica_groups=mesh['rep'=4,'shard'=8] {'shard'}, dimensions={1}, use_global_device_ids=true | all-gather | bytes 4608 | tf_op jit(solution)/shard_map/all_gather | solution.py:1133
  47.6 0.6 convert_element_type.21.gain_ref
  48.2 1.0 fusion
  49.2 1.3 pad_maximum_fusion.1
  50.5 2.0 copy.57
  52.5 14.7 %all-gather.4.cloned.1.call-done.weight_ref = bf16[1024,3072]{1,0:T(8,128)(2,1)} async-done(((bf16[128,3072]{1,0:T(8,128)(2,1)}), bf16[1024,3072]{1,0:T(8,128)(2,1)}) %all-gather.4.cloned.1.call-update) | async-done | bytes 6291472 | tf_op jit(solution)/shard_map/all_gather | solution.py:1127
  67.1 18.3 %attention_pass.1 = (bf16[512,1024]{1,0:T(8,128)(2,1)}, bf16[512,1024]{1,0:T(8,128)(2,1)}, bf16[512,512]{1,0:T(8,128)(2,1)}, bf16[512,512]{1,0:T(8,128)(2,1)}, b...) custom-call(bf16[512,1024]{1,0:T(8,128)(2,1)} %bitcast.1.arrived_ref, ...), custom_call_target="tpu_custom_call" | custom-call | flops 12884901888 | bytes 16777216 | tf_op jit(solution)/shard_map/attention_pass/pallas_call | solution.py:881
  85.4 38.1 %all-gather.6.cloned.1.call-done = bf16[4096,1024]{1,0:T(8,128)(2,1)} async-done(((bf16[512,1024]{1,0:T(8,128)(2,1)}), bf16[4096,1024]{1,0:T(8,128)(2,1)}) %all-gather.6.cloned.1.call-update) | async-done | bytes 8388624 | tf_op jit(solution)/shard_map/all_gather | solution.py:1135
  123.5 85.6 %expert_pass.1 = (bf16[8,512,1024]{2,1,0:T(8,128)(2,1)}, bf16[8,512,2048]{2,1,0:T(8,128)(2,1)}, bf16[2,1024,512]{2,1,0:T(8,128)(2,1)}, bf16[2,1024,512]{2,1,0:T(8,128)(2,1)}, bf16[2,512,1024]{2,1,0:T(8,128)(2,1)}) custom-call(bf16[512,1024]{1,0:T(8,128)(2,1)} %get-tuple-element.33.own_ref, bf16[8,8,64,1024]{3,2,1,0:T(8,128)(2,1)} %bitcast.35, ...), custom_call_target="tpu_custom_call" | custom-call | flops 51539607552 | bytes 67108864 | tf_op jit(solution)/shard_map/expert_pass/pallas_call | solution.py:215
  209.1 115.0 %return_pass.1 = (f32[512,1024]{1,0:T(8,128)}, bf16[512,1024]{1,0:T(8,128)(2,1)}) custom-call(bf16[8,512,2048]{2,1,0:T(8,128)(2,1)} %get-tuple-element.34.grad_ref, bf16[8,8,64,1024]{3,2,1,0:T(8,128)(2,1)} %bitcast.46, bf16[2,1024,512]{2,1,0:T(8,128)(2,1)} %gate_ref.3, bf16[2,1024,512]{2,1,0:T(8,128)(2,1)} %up_ref.3, bf16[2,512,1024]{2,1,0:T(8,128)(2,1)} %down_ref.3, ...), custom_call_target="tpu_custom_call" | custom-call | flops 25769803776 | bytes 67108864 | tf_op jit(solution)/shard_map/return_pass/pallas_call | solution.py:416
  324.0 2.3 constant_dynamic-slice_fusion
  326.3 35.2 %slope_pass.1 = (bf16[1024,3072]{1,0:T(8,128)(2,1)}, f32[8,1024]{1,0:T(8,128)}, bf16[512,1024]{1,0:T(8,128)(2,1)}) custom-call(f32[512,1024]{1,0:T(8,128)} %get-tuple-element.38.back_ref, bf16[512,1024]{1,0:T(8,128)(2,1)} %bitcast.32, s32[512,1]{1,0:T(8,128)} %copy.53.order_ref, s32[1,512]{1,0:T(1,128)} %bitcast.40, s32[512,1]{1,0:T(8,128)} %copy.54.column_ref, ...), custom_call_target="tpu_custom_call" | custom-call | flops 25769803776 | bytes 16777216 | tf_op jit(solution)/shard_map/slope_pass/pallas_call | solution.py:1058
  361.5 97.0 %settle_pass.1 = (f32[128,3072]{1,0:T(8,128)}, f32[8,128]{1,0:T(8,128)}, bf16[8,64,1024]{2,1,0:T(8,128)(2,1)}) custom-call(bf16[1024,3072]{1,0:T(8,128)(2,1)} %get-tuple-element.46.delta_ref, f32[8,8,128]{2,1,0:T(8,128)} %bitcast.37, bf16[8,64,1024]{2,1,0:T(8,128)(2,1)} %bitcast.31), custom_call_target="tpu_custom_call" | custom-call | flops 16777216 | bytes 67108864 | tf_op jit(solution)/shard_map/settle_pass/pallas_call | solution.py:721
  458.5 1.3 slice_bitcast_fusion
  459.8 1.9 fusion.4
  461.7 2.3 fusion.3
  463.9 4.3 convert_element_type.22
  468.3 2.6 convert_element_type.23
  470.9 2.5 convert_element_type.24
  473.4 1.0 copy.65
  474.4 0.6 copy-done.3
  475.0 1.0 copy.66
  (40 shorter events, 0.6 us)
Async XLA Ops:
  7.2 3.0 copy-start.4
  7.2 3.0 copy-start.5
  7.2 3.1 copy-start.8
  7.2 59.9 %all-gather.4.cloned.1.call-start = ((), (), s32[]{:S(2)}) async-start(), calls=%async_computation.2 | async-start | bytes 7077888 | tf_op jit(solution)/shard_map/all_gather | solution.py:1127
  9.4 8.0 %copy-start.9 = (s32[1,4]{1,0:T(1,128)S(1)}, s32[1,4]{1,0:T(1,128)}, u32[]{:S(2)}) copy-start(s32[1,4]{1,0:T(1,128)} %param.18) | copy-start | bytes 52
  9.4 8.2 %copy-start.7 = (s32[512]{0:T(512)S(1)}, s32[512]{0:T(512)}, u32[]{:S(2)}) copy-start(s32[512]{0:T(512)} %param.19) | copy-start | bytes 6148
  9.4 114.1 %all-gather.6.cloned.1.call-start = ((), (), s32[]{:S(2)}) async-start(), calls=%async_computation.3 | async-start | bytes 9437184 | tf_op jit(solution)/shard_map/all_gather | solution.py:1135
  11.4 16.0 %copy-start.10 = (bf16[128]{0:T(256)(128)(2,1)S(1)}, bf16[128]{0:T(256)(128)(2,1)}, u32[]{:S(2)}) copy-start(bf16[128]{0:T(256)(128)(2,1)} %param.28) | copy-start | bytes 772
  11.4 16.0 %copy-start.11 = (bf16[128]{0:T(256)(128)(2,1)S(1)}, bf16[128]{0:T(256)(128)(2,1)}, u32[]{:S(2)}) copy-start(bf16[128]{0:T(256)(128)(2,1)} %param.23) | copy-start | bytes 772
  12.2 10.0 %all-to-all-start.1 = ((f32[8,2,512]{2,1,0:T(2,128)}), f32[8,2,512]{2,1,0:T(2,128)S(1)}, u32[]{:S(2)}, u32[]{:S(2)}) async-start(f32[8,2,512]{2,1,0:T(2,128)} %all_to_all.16), calls=%async_computation.1 | async-start | bytes 65536 | tf_op jit(solution)/shard_map/all_to_all | solution.py:1148
  22.2 30.3 %all-to-all-start = ((bf16[8,64,1024]{2,1,0:T(8,128)(2,1)}), bf16[8,64,1024]{2,1,0:T(8,128)(2,1)}, u32[]{:S(2)}, u32[]{:S(2)}) async-start(bf16[8,64,1024]{2,1,0:T(8,128)(2,1)} %bitcast), calls=%async_computation | async-start | bytes 2097152 | tf_op jit(solution)/shard_map/all_to_all | solution.py:1123
  26.5 437.5 %all-reduce.3.cloned.1.call-start = ((), (), s32[]{:S(2)}) async-start(), calls=%async_computation.4 | async-start | bytes 12582912 | tf_op jit(solution)/shard_map/psum | solution.py:1157
  26.6 25.9 %copy-start.6 = (s32[512]{0:T(512)}, s32[512]{0:T(512)S(1)}, u32[]{:S(2)}) copy-start(s32[512]{0:T(512)S(1)} %get-tuple-element.56) | copy-start | bytes 6148
  463.9 4.4 copy-start.1
  468.3 2.6 copy-start
  470.9 2.5 copy-start.2
  473.4 1.6 copy-start.3
Sparse Core Ops, SparseCore 0:
  10.5 56.5 all-gather.3
  69.0 54.3 all-gather.5
  209.2 237.4 all-reduce.2
